TPU v7x, 256 devices: a whole 4x4x8 slice. The times are simulated.
256 devices in a mesh: section: 4 (over x), expert: 64 (over y, z, core).
Axes of the slice: x: 4, y: 4, z: 8, core: 2. Of those that a mesh axis runs over, the one named last changes fastest.
Arguments:
- tokens: bfloat16 [6, 1536, 1440], P(None, 'expert'), may hold values from -36 to 36
- norm_gain: float32 [4, 1440], P('section'), may hold values from 0.5 to 1.5
- gate_up: bfloat16 [4, 64, 1440, 2880], P('section', 'expert'), may hold values from -0.15625 to 0.15625
- down: bfloat16 [4, 64, 1440, 1440], P('section', 'expert'), may hold values from -0.15625 to 0.15625
- routes: int32 [4, 6, 1536, 4], P('section', None, 'expert'), may hold values from 0 to 63, all different within a row; in each aligned block of 24 rows (0 to 23, 24 to 47, ..., all dimensions but the last counted through in order) at most 2 rows name the same one
- route_weights: int32 [4, 6, 1536, 4], P('section', None, 'expert'), may hold values from 1 to 4095
Outputs:
- layer_outputs: bfloat16 [4, 6, 1536, 1440], P('section', None, 'expert')
Inputs may be any that keep to these rules, and one draw needn't show every extreme that they name: `routes`: each token names 4 different experts; among the 24 tokens of one index of expert in one micro-batch of one layer, no expert is named by more than 2 tokens, a bound that some block reaches.
All inputs are finite; a program needn't handle non-finite values.
Results may differ from a plain program's by a relative error of at most 0.007.
Values may be sent and summed in bfloat16 or wider, within the bound.
No kernel may reach another device: no remote copies, remote signals or barrier semaphores. Data moves between devices by JAX's collectives and lax.ppermute only.
A program may use at most 64 MiB of HBM per device.

v0:
```python
import jax
import jax.numpy as jnp
from jax import lax
from jax.sharding import PartitionSpec as P


def passed_along(value, axis, steps):
    count = lax.axis_size(axis)
    leading, last = (max(0, -steps), min(count, count - steps))
    return lax.ppermute(value, axis, [(source, source + steps) for source in range(leading, last)])


def expert_ffn(arrived, gate_up_w, down_w):
    senders, slot_count, width = arrived.shape
    hidden_units = down_w.shape[0]
    flat_rows = arrived.reshape(senders * slot_count, width)
    projected = jnp.dot(flat_rows, gate_up_w, preferred_element_type=jnp.float32)
    gate_part = projected[:, :hidden_units]
    up_part = projected[:, hidden_units:]
    activated = (gate_part * jax.nn.sigmoid(1.702 * gate_part) * (up_part + 1.0)).astype(
        jnp.bfloat16
    )
    result_rows = jnp.dot(activated, down_w, preferred_element_type=jnp.float32).astype(
        jnp.bfloat16
    )
    return result_rows.reshape(senders, slot_count, width)


def layer_step(stream, gain_row, gate_up_w, down_w, route_rows, weight_rows):
    token_count, chosen = route_rows.shape
    width = stream.shape[1]
    experts_n = lax.axis_size("expert")
    capacity = max(2, token_count * chosen * 3 // (2 * experts_n))
    widened = stream.astype(jnp.float32)
    scale = lax.rsqrt(jnp.mean(widened * widened, axis=-1, keepdims=True) + 1e-05)
    normed = (widened * scale * gain_row[None, :]).astype(jnp.bfloat16)
    flat_routes = route_rows.reshape(-1)
    matches = (flat_routes[:, None] == jnp.arange(experts_n, dtype=jnp.int32)[None, :]).astype(
        jnp.int32
    )
    slot_index = jnp.sum((jnp.cumsum(matches, axis=0) - 1) * matches, axis=1)
    target = flat_routes * capacity + slot_index
    placing = (
        jnp.arange(experts_n * capacity, dtype=jnp.int32)[:, None] == target[None, :]
    ).astype(jnp.bfloat16)
    repeated = jnp.repeat(normed, chosen, axis=0)
    outgoing = jnp.dot(placing, repeated, preferred_element_type=jnp.float32).astype(jnp.bfloat16)
    outgoing = outgoing.reshape(experts_n, capacity, width)
    arrived = lax.all_to_all(outgoing, "expert", split_axis=0, concat_axis=0, tiled=True)
    computed = expert_ffn(arrived, gate_up_w, down_w)
    returned = lax.all_to_all(computed, "expert", split_axis=0, concat_axis=0, tiled=True)
    returned_rows = returned.reshape(experts_n * capacity, width)
    gathered = jnp.take(returned_rows, target, axis=0).reshape(token_count, chosen, width)
    fixed_point = weight_rows.astype(jnp.float32)
    shares = fixed_point / jnp.sum(fixed_point, axis=-1, keepdims=True)
    accumulated = widened
    for branch in range(chosen):
        accumulated = accumulated + shares[:, branch : branch + 1] * gathered[:, branch].astype(
            jnp.float32
        )
    return accumulated.astype(jnp.bfloat16)


def shards(tokens, norm_gain, gate_up, down, routes, route_weights):
    micro_count, token_count, width = tokens.shape
    sections = lax.axis_size("section")
    section_index = lax.axis_index("section")
    gain_row = norm_gain[0]
    gate_up_w = gate_up[0, 0]
    down_w = down[0, 0]
    incoming = jnp.zeros((token_count, width), jnp.bfloat16)
    results = jnp.zeros((micro_count, token_count, width), jnp.bfloat16)
    tick_total = micro_count + sections - 1
    for tick_number in range(tick_total):
        fresh_input = tokens[min(tick_number, micro_count - 1)]
        stream = jnp.where(section_index == 0, fresh_input, incoming)
        micro_here = tick_number - section_index
        clamped = jnp.clip(micro_here, 0, micro_count - 1)
        route_rows = lax.dynamic_index_in_dim(routes[0], clamped, 0, keepdims=False)
        weight_rows = lax.dynamic_index_in_dim(route_weights[0], clamped, 0, keepdims=False)
        output_rows = layer_step(stream, gain_row, gate_up_w, down_w, route_rows, weight_rows)
        active = jnp.logical_and(micro_here >= 0, micro_here < micro_count)
        updated = lax.dynamic_update_index_in_dim(results, output_rows, clamped, 0)
        results = jnp.where(active, updated, results)
        if tick_number + 1 < tick_total:
            incoming = passed_along(output_rows, "section", 1)
    return results[None]


def solution(mesh):
    return jax.shard_map(
        shards,
        mesh=mesh,
        in_specs=(
            P(None, "expert", None),
            P("section", None),
            P("section", "expert", None, None),
            P("section", "expert", None, None),
            P("section", None, "expert", None),
            P("section", None, "expert", None),
        ),
        out_specs=P("section", None, "expert", None),
        check_vma=False,
    )
```

profile of v0, /device:TPU:1, one launch (start us, length us, event | category | flops | bytes accessed | tf_op | source)
XLA Modules:
  0.0 579.2 jit_solution(16545777119109301416)
XLA Ops:
  5.8 13.1 %all-to-all-start = ((bf16[64,2,1440]{2,1,0:T(2,128)(2,1)}), bf16[64,2,1440]{2,1,0:T(2,128)(2,1)S(1)}, u32[]{:S(2)}, u32[]{:S(2)}) async-start(bf16[64,2,1440]{2,1,0:T(2,128)(2,1)} %reshape.672), calls=%async_computation | async-start | bytes 786432 | tf_op jit(solution)/shard_map/all_to_all | solution.py:49
  19.5 14.0 %all-to-all-done = bf16[64,2,1440]{2,1,0:T(2,128)(2,1)S(1)} async-done(((bf16[64,2,1440]{2,1,0:T(2,128)(2,1)}), bf16[64,2,1440]{2,1,0:T(2,128)(2,1)S(1)}, u32[]{:S(2)}, u32[]{:S(2)}) %all-to-all-start) | async-done | bytes 368672 | tf_op jit(solution)/shard_map/all_to_all | solution.py:49
  33.8 7.0 %fusion.16 = f32[128,2880]{0,1:T(8,128)S(1)} fusion(bf16[128,1440]{1,0:T(8,128)(2,1)S(1)} %reshape.673, bf16[1,1,1440,2880]{3,2,1,0:T(8,128)(2,1)} %param.10), kind=kOutput, calls=%fused_computation.25 | convolution fusion | flops 1061683200 | bytes 10137600 | tf_op jit(solution)/shard_map/dot_general | solution.py:17
  53.1 13.8 %all-to-all-done.1 = bf16[64,2,1440]{2,1,0:T(2,128)(2,1)S(1)} async-done(((bf16[64,2,1440]{2,1,0:T(2,128)(2,1)}), bf16[64,2,1440]{2,1,0:T(2,128)(2,1)S(1)}, u32[]{:S(2)}, u32[]{:S(2)}) %all-to-all-start.1) | async-done | bytes 368672 | tf_op jit(solution)/shard_map/all_to_all | solution.py:51
  75.1 7.1 %all-to-all-start.2 = ((bf16[64,2,1440]{2,1,0:T(2,128)(2,1)}), bf16[64,2,1440]{2,1,0:T(2,128)(2,1)S(1)}, u32[]{:S(2)}, u32[]{:S(2)}) async-start(bf16[64,2,1440]{2,1,0:T(2,128)(2,1)} %reshape.679), calls=%async_computation.2 | async-start | bytes 786432 | tf_op jit(solution)/shard_map/all_to_all | solution.py:49
  82.2 14.5 %all-to-all-done.2 = bf16[64,2,1440]{2,1,0:T(2,128)(2,1)S(1)} async-done(((bf16[64,2,1440]{2,1,0:T(2,128)(2,1)}), bf16[64,2,1440]{2,1,0:T(2,128)(2,1)S(1)}, u32[]{:S(2)}, u32[]{:S(2)}) %all-to-all-start.2) | async-done | bytes 368672 | tf_op jit(solution)/shard_map/all_to_all | solution.py:49
  97.0 7.0 %fusion.14 = f32[128,2880]{0,1:T(8,128)S(1)} fusion(bf16[128,1440]{1,0:T(8,128)(2,1)S(1)} %reshape.680, bf16[1,1,1440,2880]{3,2,1,0:T(8,128)(2,1)} %param.10), kind=kOutput, calls=%fused_computation.23 | convolution fusion | flops 1061683200 | bytes 10137600 | tf_op jit(solution)/shard_map/dot_general | solution.py:17
  115.8 14.3 %all-to-all-done.3 = bf16[64,2,1440]{2,1,0:T(2,128)(2,1)S(1)} async-done(((bf16[64,2,1440]{2,1,0:T(2,128)(2,1)}), bf16[64,2,1440]{2,1,0:T(2,128)(2,1)S(1)}, u32[]{:S(2)}, u32[]{:S(2)}) %all-to-all-start.3) | async-done | bytes 368672 | tf_op jit(solution)/shard_map/all_to_all | solution.py:51
  139.2 7.1 %all-to-all-start.4 = ((bf16[64,2,1440]{2,1,0:T(2,128)(2,1)}), bf16[64,2,1440]{2,1,0:T(2,128)(2,1)S(1)}, u32[]{:S(2)}, u32[]{:S(2)}) async-start(bf16[64,2,1440]{2,1,0:T(2,128)(2,1)} %reshape.686), calls=%async_computation.4 | async-start | bytes 786432 | tf_op jit(solution)/shard_map/all_to_all | solution.py:49
  147.1 13.7 %all-to-all-done.4 = bf16[64,2,1440]{2,1,0:T(2,128)(2,1)S(1)} async-done(((bf16[64,2,1440]{2,1,0:T(2,128)(2,1)}), bf16[64,2,1440]{2,1,0:T(2,128)(2,1)S(1)}, u32[]{:S(2)}, u32[]{:S(2)}) %all-to-all-start.4) | async-done | bytes 368672 | tf_op jit(solution)/shard_map/all_to_all | solution.py:49
  161.1 7.0 %fusion.12 = f32[128,2880]{0,1:T(8,128)S(1)} fusion(bf16[128,1440]{1,0:T(8,128)(2,1)S(1)} %reshape.687, bf16[1,1,1440,2880]{3,2,1,0:T(8,128)(2,1)} %param.10), kind=kOutput, calls=%fused_computation.21 | convolution fusion | flops 1061683200 | bytes 10137600 | tf_op jit(solution)/shard_map/dot_general | solution.py:17
  180.0 14.2 %all-to-all-done.5 = bf16[64,2,1440]{2,1,0:T(2,128)(2,1)S(1)} async-done(((bf16[64,2,1440]{2,1,0:T(2,128)(2,1)}), bf16[64,2,1440]{2,1,0:T(2,128)(2,1)S(1)}, u32[]{:S(2)}, u32[]{:S(2)}) %all-to-all-start.5) | async-done | bytes 368672 | tf_op jit(solution)/shard_map/all_to_all | solution.py:51
  202.6 21.6 %all_to_all.90 = bf16[64,2,1440]{2,1,0:T(2,128)(2,1)S(1)} all-to-all(bf16[64,2,1440]{2,1,0:T(2,128)(2,1)S(1)} %reshape.693), channel_id=1, replica_groups=mesh['section'=4,'expert'=64] {'expert'}, dimensions={0} | all-to-all | bytes 737280 | tf_op jit(solution)/shard_map/all_to_all | solution.py:49
  224.4 7.0 %fusion.10 = f32[128,2880]{0,1:T(8,128)S(1)} fusion(bf16[128,1440]{1,0:T(8,128)(2,1)S(1)} %reshape.694, bf16[1,1,1440,2880]{3,2,1,0:T(8,128)(2,1)} %param.10), kind=kOutput, calls=%fused_computation.19 | convolution fusion | flops 1061683200 | bytes 10137600 | tf_op jit(solution)/shard_map/dot_general | solution.py:17
  243.0 14.5 %all-to-all-done.7 = bf16[64,2,1440]{2,1,0:T(2,128)(2,1)S(1)} async-done(((bf16[64,2,1440]{2,1,0:T(2,128)(2,1)}), bf16[64,2,1440]{2,1,0:T(2,128)(2,1)S(1)}, u32[]{:S(2)}, u32[]{:S(2)}) %all-to-all-start.7) | async-done | bytes 368672 | tf_op jit(solution)/shard_map/all_to_all | solution.py:51
  266.6 7.4 %all-to-all-start.8 = ((bf16[64,2,1440]{2,1,0:T(2,128)(2,1)}), bf16[64,2,1440]{2,1,0:T(2,128)(2,1)S(1)}, u32[]{:S(2)}, u32[]{:S(2)}) async-start(bf16[64,2,1440]{2,1,0:T(2,128)(2,1)} %reshape.700), calls=%async_computation.8 | async-start | bytes 786432 | tf_op jit(solution)/shard_map/all_to_all | solution.py:49
  274.8 13.6 %all-to-all-done.8 = bf16[64,2,1440]{2,1,0:T(2,128)(2,1)S(1)} async-done(((bf16[64,2,1440]{2,1,0:T(2,128)(2,1)}), bf16[64,2,1440]{2,1,0:T(2,128)(2,1)S(1)}, u32[]{:S(2)}, u32[]{:S(2)}) %all-to-all-start.8) | async-done | bytes 368672 | tf_op jit(solution)/shard_map/all_to_all | solution.py:49
  288.7 7.0 %fusion.8 = f32[128,2880]{0,1:T(8,128)S(1)} fusion(bf16[128,1440]{1,0:T(8,128)(2,1)S(1)} %reshape.701, bf16[1,1,1440,2880]{3,2,1,0:T(8,128)(2,1)} %param.10), kind=kOutput, calls=%fused_computation.17 | convolution fusion | flops 1061683200 | bytes 10137600 | tf_op jit(solution)/shard_map/dot_general | solution.py:17
  307.6 14.2 %all-to-all-done.9 = bf16[64,2,1440]{2,1,0:T(2,128)(2,1)S(1)} async-done(((bf16[64,2,1440]{2,1,0:T(2,128)(2,1)}), bf16[64,2,1440]{2,1,0:T(2,128)(2,1)S(1)}, u32[]{:S(2)}, u32[]{:S(2)}) %all-to-all-start.9) | async-done | bytes 368672 | tf_op jit(solution)/shard_map/all_to_all | solution.py:51
  330.2 21.9 %all_to_all.91 = bf16[64,2,1440]{2,1,0:T(2,128)(2,1)S(1)} all-to-all(bf16[64,2,1440]{2,1,0:T(2,128)(2,1)S(1)} %reshape.707), channel_id=1, replica_groups=mesh['section'=4,'expert'=64] {'expert'}, dimensions={0} | all-to-all | bytes 737280 | tf_op jit(solution)/shard_map/all_to_all | solution.py:49
  352.3 7.0 %fusion.6 = f32[128,2880]{0,1:T(8,128)S(1)} fusion(bf16[128,1440]{1,0:T(8,128)(2,1)S(1)} %reshape.708, bf16[1,1,1440,2880]{3,2,1,0:T(8,128)(2,1)} %param.10), kind=kOutput, calls=%fused_computation.15 | convolution fusion | flops 1061683200 | bytes 10137600 | tf_op jit(solution)/shard_map/dot_general | solution.py:17
  370.8 14.5 %all-to-all-done.11 = bf16[64,2,1440]{2,1,0:T(2,128)(2,1)S(1)} async-done(((bf16[64,2,1440]{2,1,0:T(2,128)(2,1)}), bf16[64,2,1440]{2,1,0:T(2,128)(2,1)S(1)}, u32[]{:S(2)}, u32[]{:S(2)}) %all-to-all-start.11) | async-done | bytes 368672 | tf_op jit(solution)/shard_map/all_to_all | solution.py:51
  394.4 7.4 %all-to-all-start.12 = ((bf16[64,2,1440]{2,1,0:T(2,128)(2,1)}), bf16[64,2,1440]{2,1,0:T(2,128)(2,1)S(1)}, u32[]{:S(2)}, u32[]{:S(2)}) async-start(bf16[64,2,1440]{2,1,0:T(2,128)(2,1)} %reshape.714), calls=%async_computation.12 | async-start | bytes 786432 | tf_op jit(solution)/shard_map/all_to_all | solution.py:49
  402.6 13.6 %all-to-all-done.12 = bf16[64,2,1440]{2,1,0:T(2,128)(2,1)S(1)} async-done(((bf16[64,2,1440]{2,1,0:T(2,128)(2,1)}), bf16[64,2,1440]{2,1,0:T(2,128)(2,1)S(1)}, u32[]{:S(2)}, u32[]{:S(2)}) %all-to-all-start.12) | async-done | bytes 368672 | tf_op jit(solution)/shard_map/all_to_all | solution.py:49
  416.5 7.0 %fusion.4 = f32[128,2880]{0,1:T(8,128)S(1)} fusion(bf16[128,1440]{1,0:T(8,128)(2,1)S(1)} %reshape.715, bf16[1,1,1440,2880]{3,2,1,0:T(8,128)(2,1)} %param.10), kind=kOutput, calls=%fused_computation.13 | convolution fusion | flops 1061683200 | bytes 10137600 | tf_op jit(solution)/shard_map/dot_general | solution.py:17
  435.4 14.2 %all-to-all-done.13 = bf16[64,2,1440]{2,1,0:T(2,128)(2,1)S(1)} async-done(((bf16[64,2,1440]{2,1,0:T(2,128)(2,1)}), bf16[64,2,1440]{2,1,0:T(2,128)(2,1)S(1)}, u32[]{:S(2)}, u32[]{:S(2)}) %all-to-all-start.13) | async-done | bytes 368672 | tf_op jit(solution)/shard_map/all_to_all | solution.py:51
  458.0 21.7 %all_to_all.92 = bf16[64,2,1440]{2,1,0:T(2,128)(2,1)S(1)} all-to-all(bf16[64,2,1440]{2,1,0:T(2,128)(2,1)S(1)} %reshape.721), channel_id=1, replica_groups=mesh['section'=4,'expert'=64] {'expert'}, dimensions={0} | all-to-all | bytes 737280 | tf_op jit(solution)/shard_map/all_to_all | solution.py:49
  479.9 7.0 %fusion.2 = f32[128,2880]{0,1:T(8,128)S(1)} fusion(bf16[128,1440]{1,0:T(8,128)(2,1)S(1)} %reshape.722, bf16[1,1,1440,2880]{3,2,1,0:T(8,128)(2,1)} %param.10), kind=kOutput, calls=%fused_computation.11 | convolution fusion | flops 1061683200 | bytes 10137600 | tf_op jit(solution)/shard_map/dot_general | solution.py:17
  498.4 14.5 %all-to-all-done.15 = bf16[64,2,1440]{2,1,0:T(2,128)(2,1)S(1)} async-done(((bf16[64,2,1440]{2,1,0:T(2,128)(2,1)}), bf16[64,2,1440]{2,1,0:T(2,128)(2,1)S(1)}, u32[]{:S(2)}, u32[]{:S(2)}) %all-to-all-start.15) | async-done | bytes 368672 | tf_op jit(solution)/shard_map/all_to_all | solution.py:51
  521.3 21.7 %all_to_all.93 = bf16[64,2,1440]{2,1,0:T(2,128)(2,1)S(1)} all-to-all(bf16[64,2,1440]{2,1,0:T(2,128)(2,1)S(1)} %reshape.728), channel_id=1, replica_groups=mesh['section'=4,'expert'=64] {'expert'}, dimensions={0} | all-to-all | bytes 737280 | tf_op jit(solution)/shard_map/all_to_all | solution.py:49
  543.3 7.0 %fusion = f32[128,2880]{0,1:T(8,128)S(1)} fusion(bf16[128,1440]{1,0:T(8,128)(2,1)S(1)} %reshape.729, bf16[1,1,1440,2880]{3,2,1,0:T(8,128)(2,1)} %param.10), kind=kOutput, calls=%fused_computation.9 | convolution fusion | flops 1061683200 | bytes 10137600 | tf_op jit(solution)/shard_map/dot_general | solution.py:17
  562.6 13.7 %all-to-all-done.17 = bf16[64,2,1440]{2,1,0:T(2,128)(2,1)S(1)} async-done(((bf16[64,2,1440]{2,1,0:T(2,128)(2,1)}), bf16[64,2,1440]{2,1,0:T(2,128)(2,1)S(1)}, u32[]{:S(2)}, u32[]{:S(2)}) %all-to-all-start.17) | async-done | bytes 368672 | tf_op jit(solution)/shard_map/all_to_all | solution.py:51
  (275 shorter events, 188.0 us)
Async XLA Ops:
  5.8 27.7 %all-to-all-start = ((bf16[64,2,1440]{2,1,0:T(2,128)(2,1)}), bf16[64,2,1440]{2,1,0:T(2,128)(2,1)S(1)}, u32[]{:S(2)}, u32[]{:S(2)}) async-start(bf16[64,2,1440]{2,1,0:T(2,128)(2,1)} %reshape.672), calls=%async_computation | async-start | bytes 786432 | tf_op jit(solution)/shard_map/all_to_all | solution.py:49
  40.8 11.8 %copy-start.1 = (s32[1,6,24,4]{2,3,1,0:T(4,128)S(1)}, s32[1,6,24,4]{2,3,1,0:T(4,128)}, u32[]{:S(2)}) copy-start(s32[1,6,24,4]{2,3,1,0:T(4,128)} %param.13) | copy-start | bytes 6916
  45.0 23.6 %copy-start = (bf16[6,24,1440]{2,1,0:T(8,128)(2,1)S(1)}, bf16[6,24,1440]{2,1,0:T(8,128)(2,1)}, u32[]{:S(2)}) copy-start(bf16[6,24,1440]{2,1,0:T(8,128)(2,1)} %param.8) | copy-start | bytes 1244164
  46.1 20.8 %all-to-all-start.1 = ((bf16[64,2,1440]{2,1,0:T(2,128)(2,1)}), bf16[64,2,1440]{2,1,0:T(2,128)(2,1)S(1)}, u32[]{:S(2)}, u32[]{:S(2)}) async-start(bf16[64,2,1440]{2,1,0:T(2,128)(2,1)} %reshape.674), calls=%async_computation.1 | async-start | bytes 786432 | tf_op jit(solution)/shard_map/all_to_all | solution.py:51
  68.8 4.5 collective-permute-start
  75.1 21.6 %all-to-all-start.2 = ((bf16[64,2,1440]{2,1,0:T(2,128)(2,1)}), bf16[64,2,1440]{2,1,0:T(2,128)(2,1)S(1)}, u32[]{:S(2)}, u32[]{:S(2)}) async-start(bf16[64,2,1440]{2,1,0:T(2,128)(2,1)} %reshape.679), calls=%async_computation.2 | async-start | bytes 786432 | tf_op jit(solution)/shard_map/all_to_all | solution.py:49
  109.3 20.8 %all-to-all-start.3 = ((bf16[64,2,1440]{2,1,0:T(2,128)(2,1)}), bf16[64,2,1440]{2,1,0:T(2,128)(2,1)S(1)}, u32[]{:S(2)}, u32[]{:S(2)}) async-start(bf16[64,2,1440]{2,1,0:T(2,128)(2,1)} %reshape.681), calls=%async_computation.3 | async-start | bytes 786432 | tf_op jit(solution)/shard_map/all_to_all | solution.py:51
  131.9 5.4 collective-permute-start.1
  139.2 21.6 %all-to-all-start.4 = ((bf16[64,2,1440]{2,1,0:T(2,128)(2,1)}), bf16[64,2,1440]{2,1,0:T(2,128)(2,1)S(1)}, u32[]{:S(2)}, u32[]{:S(2)}) async-start(bf16[64,2,1440]{2,1,0:T(2,128)(2,1)} %reshape.686), calls=%async_computation.4 | async-start | bytes 786432 | tf_op jit(solution)/shard_map/all_to_all | solution.py:49
  173.4 20.8 %all-to-all-start.5 = ((bf16[64,2,1440]{2,1,0:T(2,128)(2,1)}), bf16[64,2,1440]{2,1,0:T(2,128)(2,1)S(1)}, u32[]{:S(2)}, u32[]{:S(2)}) async-start(bf16[64,2,1440]{2,1,0:T(2,128)(2,1)} %reshape.688), calls=%async_computation.5 | async-start | bytes 786432 | tf_op jit(solution)/shard_map/all_to_all | solution.py:51
  196.0 5.4 collective-permute-start.2
  236.7 20.8 %all-to-all-start.7 = ((bf16[64,2,1440]{2,1,0:T(2,128)(2,1)}), bf16[64,2,1440]{2,1,0:T(2,128)(2,1)S(1)}, u32[]{:S(2)}, u32[]{:S(2)}) async-start(bf16[64,2,1440]{2,1,0:T(2,128)(2,1)} %reshape.695), calls=%async_computation.7 | async-start | bytes 786432 | tf_op jit(solution)/shard_map/all_to_all | solution.py:51
  259.3 5.4 collective-permute-start.3
  266.6 21.9 %all-to-all-start.8 = ((bf16[64,2,1440]{2,1,0:T(2,128)(2,1)}), bf16[64,2,1440]{2,1,0:T(2,128)(2,1)S(1)}, u32[]{:S(2)}, u32[]{:S(2)}) async-start(bf16[64,2,1440]{2,1,0:T(2,128)(2,1)} %reshape.700), calls=%async_computation.8 | async-start | bytes 786432 | tf_op jit(solution)/shard_map/all_to_all | solution.py:49
  301.0 20.8 %all-to-all-start.9 = ((bf16[64,2,1440]{2,1,0:T(2,128)(2,1)}), bf16[64,2,1440]{2,1,0:T(2,128)(2,1)S(1)}, u32[]{:S(2)}, u32[]{:S(2)}) async-start(bf16[64,2,1440]{2,1,0:T(2,128)(2,1)} %reshape.702), calls=%async_computation.9 | async-start | bytes 786432 | tf_op jit(solution)/shard_map/all_to_all | solution.py:51
  323.6 5.4 collective-permute-start.4
  364.6 20.8 %all-to-all-start.11 = ((bf16[64,2,1440]{2,1,0:T(2,128)(2,1)}), bf16[64,2,1440]{2,1,0:T(2,128)(2,1)S(1)}, u32[]{:S(2)}, u32[]{:S(2)}) async-start(bf16[64,2,1440]{2,1,0:T(2,128)(2,1)} %reshape.709), calls=%async_computation.11 | async-start | bytes 786432 | tf_op jit(solution)/shard_map/all_to_all | solution.py:51
  387.2 5.4 collective-permute-start.5
  394.4 21.8 %all-to-all-start.12 = ((bf16[64,2,1440]{2,1,0:T(2,128)(2,1)}), bf16[64,2,1440]{2,1,0:T(2,128)(2,1)S(1)}, u32[]{:S(2)}, u32[]{:S(2)}) async-start(bf16[64,2,1440]{2,1,0:T(2,128)(2,1)} %reshape.714), calls=%async_computation.12 | async-start | bytes 786432 | tf_op jit(solution)/shard_map/all_to_all | solution.py:49
  428.8 20.8 %all-to-all-start.13 = ((bf16[64,2,1440]{2,1,0:T(2,128)(2,1)}), bf16[64,2,1440]{2,1,0:T(2,128)(2,1)S(1)}, u32[]{:S(2)}, u32[]{:S(2)}) async-start(bf16[64,2,1440]{2,1,0:T(2,128)(2,1)} %reshape.716), calls=%async_computation.13 | async-start | bytes 786432 | tf_op jit(solution)/shard_map/all_to_all | solution.py:51
  451.4 5.4 collective-permute-start.6
  492.2 20.8 %all-to-all-start.15 = ((bf16[64,2,1440]{2,1,0:T(2,128)(2,1)}), bf16[64,2,1440]{2,1,0:T(2,128)(2,1)S(1)}, u32[]{:S(2)}, u32[]{:S(2)}) async-start(bf16[64,2,1440]{2,1,0:T(2,128)(2,1)} %reshape.723), calls=%async_computation.15 | async-start | bytes 786432 | tf_op jit(solution)/shard_map/all_to_all | solution.py:51
  514.8 5.4 collective-permute-start.7
  555.5 20.8 %all-to-all-start.17 = ((bf16[64,2,1440]{2,1,0:T(2,128)(2,1)}), bf16[64,2,1440]{2,1,0:T(2,128)(2,1)S(1)}, u32[]{:S(2)}, u32[]{:S(2)}) async-start(bf16[64,2,1440]{2,1,0:T(2,128)(2,1)} %reshape.730), calls=%async_computation.17 | async-start | bytes 786432 | tf_op jit(solution)/shard_map/all_to_all | solution.py:51
where the time goes:
time: 589 us; the launch traced here: 579 us
  waiting for transfers between devices  208 us (35%)
  starting transfers between devices  129 us (22%)
  matrix products  103 us (17%)
  blocking collectives  86.9 us (15%)
  local copies, waits for them, and re-layouts  38.1 us (6%)
  other arithmetic  11.4 us (2%)
    all_to_all x9, waiting for transfers between devices, layer_step(): lax.all_to_all(computed, 'expert', split_axis=0, concat_axis=0, tiled=True)  128 us
    all_to_all x4, blocking collectives, layer_step(): lax.all_to_all(outgoing, 'expert', split_axis=0, concat_axis=0, tiled=True)  86.9 us
    all_to_all x5, waiting for transfers between devices, layer_step(): lax.all_to_all(outgoing, 'expert', split_axis=0, concat_axis=0, tiled=True)  69.5 us
    dot_general x9, matrix products, expert_ffn(): jnp.dot(flat_rows, gate_up_w, preferred_element_type=jnp.float32)  63 us
    all_to_all x9, starting transfers between devices, layer_step(): lax.all_to_all(computed, 'expert', split_axis=0, concat_axis=0, tiled=True)  56 us
    all_to_all x5, starting transfers between devices, layer_step(): lax.all_to_all(outgoing, 'expert', split_axis=0, concat_axis=0, tiled=True)  42.1 us
    dot_general x9, matrix products, expert_ffn(): jnp.dot(activated, down_w, preferred_element_type=jnp.float32)  37.6 us
    ppermute x8, starting transfers between devices, passed_along(): lax.ppermute(value, axis, [(source, source + steps) for source in range(l...  31.3 us
  transfers between devices with their start and end apart: 22, of which 22 were waited for; matrix products, arithmetic and copies ran while one was open for 1% of the time, Pallas kernels for 0%

commit v1 on v0

v1 whole, which is shorter than its diff:
```python
import jax
import jax.numpy as jnp
from jax import lax
from jax.sharding import PartitionSpec as P

CHUNK = 2


def split_three(value):
    high = lax.reduce_precision(value, 8, 7)
    middle = lax.reduce_precision(value - high, 8, 7)
    low = value - high - middle
    return [part.astype(jnp.bfloat16) for part in (high, middle, low)]


def expert_ffn(rows, gate_up_w, down_w):
    hidden_units = down_w.shape[0]
    projected = jnp.dot(rows, gate_up_w, preferred_element_type=jnp.float32)
    gate_part = projected[:, :hidden_units]
    up_part = projected[:, hidden_units:]
    activated = (gate_part * jax.nn.sigmoid(1.702 * gate_part) * (up_part + 1.0)).astype(
        jnp.bfloat16
    )
    return jnp.dot(activated, down_w, preferred_element_type=jnp.float32).astype(jnp.bfloat16)


def shards(tokens, norm_gain, gate_up, down, routes, route_weights):
    micro_count, token_count, width = tokens.shape
    chosen = routes.shape[-1]
    experts_n = lax.axis_size("expert")
    sections = lax.axis_size("section")
    section_index = lax.axis_index("section")
    chunk_count = micro_count // CHUNK
    rows_n = CHUNK * token_count
    cap = max(2, token_count * chosen * 3 // (2 * experts_n))
    per_expert = CHUNK * cap
    slots = experts_n * per_expert
    gain_row = norm_gain[0]
    gate_up_w = gate_up[0, 0]
    down_w = down[0, 0]

    pairs = routes[0].reshape(micro_count, token_count * chosen)
    order = jnp.arange(token_count * chosen, dtype=jnp.int32)
    same = (pairs[:, :, None] == pairs[:, None, :]) & (order[None, :] < order[:, None])[None]
    rank = jnp.sum(same.astype(jnp.int32), axis=-1)
    block = (jnp.arange(micro_count, dtype=jnp.int32) % CHUNK)[:, None]
    target = (pairs * per_expert + block * cap + rank).reshape(chunk_count, rows_n, chosen)
    fixed_point = route_weights[0].astype(jnp.float32)
    shares = fixed_point / jnp.sum(fixed_point, axis=-1, keepdims=True)
    shares = shares.reshape(chunk_count, rows_n, chosen)
    chunks = tokens.reshape(chunk_count, rows_n, width)

    incoming = jnp.zeros((rows_n, width), jnp.bfloat16)
    results = jnp.zeros((chunk_count, rows_n, width), jnp.bfloat16)
    tick_total = chunk_count + sections - 1
    for tick_number in range(tick_total):
        fresh_input = chunks[min(tick_number, chunk_count - 1)]
        stream = jnp.where(section_index == 0, fresh_input, incoming)
        chunk_here = tick_number - section_index
        clamped = jnp.clip(chunk_here, 0, chunk_count - 1)
        target_rows = lax.dynamic_index_in_dim(target, clamped, 0, keepdims=False)
        share_rows = lax.dynamic_index_in_dim(shares, clamped, 0, keepdims=False)

        slot_ids = jnp.arange(slots, dtype=jnp.int32)
        hits = [slot_ids[:, None] == target_rows[None, :, k] for k in range(chosen)]
        placing = sum(h.astype(jnp.float32) for h in hits).astype(jnp.bfloat16)
        mixing = sum(
            jnp.where(slot_ids[None, :] == target_rows[:, k : k + 1], share_rows[:, k : k + 1], 0.0)
            for k in range(chosen)
        )
        mixing = jnp.concatenate(split_three(mixing), axis=0)

        widened = stream.astype(jnp.float32)
        scale = lax.rsqrt(jnp.mean(widened * widened, axis=-1, keepdims=True) + 1e-05)
        normed = (widened * scale * gain_row[None, :]).astype(jnp.bfloat16)
        outgoing = jnp.dot(placing, normed, preferred_element_type=jnp.float32).astype(jnp.bfloat16)
        outgoing = outgoing.reshape(experts_n, per_expert, width)
        arrived = lax.all_to_all(outgoing, "expert", split_axis=0, concat_axis=0, tiled=True)
        computed = expert_ffn(arrived.reshape(slots, width), gate_up_w, down_w)
        computed = computed.reshape(experts_n, per_expert, width)
        returned = lax.all_to_all(computed, "expert", split_axis=0, concat_axis=0, tiled=True)
        returned_rows = returned.reshape(slots, width)
        mixed = jnp.dot(mixing, returned_rows, preferred_element_type=jnp.float32)
        mixed = mixed.reshape(3, rows_n, width)
        output_rows = (widened + (mixed[0] + (mixed[1] + mixed[2]))).astype(jnp.bfloat16)

        active = jnp.logical_and(chunk_here >= 0, chunk_here < chunk_count)
        kept = lax.dynamic_index_in_dim(results, clamped, 0, keepdims=False)
        results = lax.dynamic_update_index_in_dim(
            results, jnp.where(active, output_rows, kept), clamped, 0
        )
        if tick_number + 1 < tick_total:
            incoming = lax.ppermute(
                output_rows, "section", [(s, s + 1) for s in range(sections - 1)]
            )
    return results.reshape(1, micro_count, token_count, width)


def solution(mesh):
    return jax.shard_map(
        shards,
        mesh=mesh,
        in_specs=(
            P(None, "expert", None),
            P("section", None),
            P("section", "expert", None, None),
            P("section", "expert", None, None),
            P("section", None, "expert", None),
            P("section", None, "expert", None),
        ),
        out_specs=P("section", None, "expert", None),
        check_vma=False,
    )
```

time: 589 us -> 500 us (0.85)
  blocking collectives: 86.9 us -> 184 us
  starting transfers between devices: 129 us -> 57 us
  waiting for transfers between devices: 208 us -> 150 us
  matrix products: 103 us -> 74.3 us
  local copies, waits for them, and re-layouts: 38.1 us -> 17.9 us
    all_to_all x4 -> x6, blocking collectives: 86.9 us -> 184 us  [shards(): lax.all_to_all(outgoing, 'expert', split_axis=0, concat_axis=0, tiled=True)]
    all_to_all x14 -> x6, waiting for transfers between devices: 197 us -> 136 us  [shards(): lax.all_to_all(computed, 'expert', split_axis=0, concat_axis=0, tiled=True)]
    all_to_all x14 -> x6, starting transfers between devices: 98.1 us -> 37.2 us  [shards(): lax.all_to_all(computed, 'expert', split_axis=0, concat_axis=0, tiled=True)]
    dot_general x18, matrix products: 65.8 us -> 48.1 us  [the longest x6 43.5 us: expert_ffn(): projected = jnp.dot(rows, gate_up_w, preferred_element_type=jnp.float32)]
    ppermute x8 -> x5, starting transfers between devices: 31.3 us -> 19.8 us  [shards(): lax.ppermute(output_rows, 'section', [(s, s + 1) for s in range(sections...]
    dot_general x9 -> x6, matrix products: 37.6 us -> 26.3 us  [expert_ffn(): jnp.dot(activated, down_w, preferred_element_type=jnp.float32)]
    reshape x63 -> x24, local copies, waits for them, and re-layouts: 20.5 us -> 12 us  [the longest x6 6.42 us: shards(): computed = computed.reshape(experts_n, per_expert, width)]
    gather x9 -> x0, local copies, waits for them, and re-layouts: 7.27 us -> none  [layer_step(): jnp.take(returned_rows, target, axis=0).reshape(token_count, chosen, width)]
  transfers between devices with their start and end apart: 22 -> 11, of which waited for: 22 -> 11; matrix products, arithmetic and copies ran while one was open for 1% -> 0% of each run, Pallas kernels for 0% -> 0%
where the time goes in v1:
time: 500 us; the launch traced here: 491 us
  blocking collectives  184 us (37%)
  waiting for transfers between devices  150 us (30%)
  matrix products  74.3 us (15%)
  starting transfers between devices  57 us (11%)
  local copies, waits for them, and re-layouts  17.9 us (4%)
  other arithmetic  6.05 us (1%)
    all_to_all x6, blocking collectives, shards(): lax.all_to_all(outgoing, 'expert', split_axis=0, concat_axis=0, tiled=True)  184 us
    all_to_all x6, waiting for transfers between devices, shards(): lax.all_to_all(computed, 'expert', split_axis=0, concat_axis=0, tiled=True)  136 us
    dot_general x6, matrix products, expert_ffn(): projected = jnp.dot(rows, gate_up_w, preferred_element_type=jnp.float32)  43.5 us
    all_to_all x6, starting transfers between devices, shards(): lax.all_to_all(computed, 'expert', split_axis=0, concat_axis=0, tiled=True)  37.2 us
    dot_general x6, matrix products, expert_ffn(): jnp.dot(activated, down_w, preferred_element_type=jnp.float32)  26.3 us
    ppermute x5, starting transfers between devices, shards(): lax.ppermute(output_rows, 'section', [(s, s + 1) for s in range(sections...  19.8 us
    ppermute x5, waiting for transfers between devices, shards(): lax.ppermute(output_rows, 'section', [(s, s + 1) for s in range(sections...  13.6 us
  transfers between devices with their start and end apart: 11, of which 11 were waited for; matrix products, arithmetic and copies ran while one was open for 0% of the time, Pallas kernels for 0%

profile of v1, /device:TPU:1, one launch (start us, length us, event | category | flops | bytes accessed | tf_op | source)
XLA Modules:
  0.0 490.9 jit_solution(11142312123306754845)
XLA Ops:
  6.2 35.9 %all_to_all.60 = bf16[64,4,1440]{2,1,0:T(4,128)(2,1)S(1)} all-to-all(bf16[64,4,1440]{2,1,0:T(4,128)(2,1)S(1)} %reshape.262), channel_id=1, replica_groups=mesh['section'=4,'expert'=64] {'expert'}, dimensions={0} | all-to-all | bytes 1474560 | tf_op jit(solution)/shard_map/all_to_all | solution.py:78
  42.5 7.3 %fusion.10 = f32[256,2880]{0,1:T(8,128)S(1)} fusion(bf16[256,1440]{1,0:T(8,128)(2,1)S(1)} %reshape.263, bf16[1,1,1440,2880]{3,2,1,0:T(8,128)(2,1)} %param.8), kind=kOutput, calls=%fused_computation.10 | convolution fusion | flops 2123366400 | bytes 11980800 | tf_op jit(solution)/shard_map/dot_general | solution.py:18
  49.8 4.4 fusion.24
  55.5 6.2 %all-to-all-start.1 = ((bf16[64,4,1440]{2,1,0:T(4,128)(2,1)}), bf16[64,4,1440]{2,1,0:T(4,128)(2,1)S(1)}, u32[]{:S(2)}, u32[]{:S(2)}) async-start(bf16[64,4,1440]{2,1,0:T(4,128)(2,1)} %reshape.264), calls=%async_computation.1 | async-start | bytes 1572864 | tf_op jit(solution)/shard_map/all_to_all | solution.py:81
  62.2 22.5 %all-to-all-done.1 = bf16[64,4,1440]{2,1,0:T(4,128)(2,1)S(1)} async-done(((bf16[64,4,1440]{2,1,0:T(4,128)(2,1)}), bf16[64,4,1440]{2,1,0:T(4,128)(2,1)S(1)}, u32[]{:S(2)}, u32[]{:S(2)}) %all-to-all-start.1) | async-done | bytes 737312 | tf_op jit(solution)/shard_map/all_to_all | solution.py:81
  92.5 29.6 %all_to_all.61 = bf16[64,4,1440]{2,1,0:T(4,128)(2,1)S(1)} all-to-all(bf16[64,4,1440]{2,1,0:T(4,128)(2,1)S(1)} %reshape.266), channel_id=1, replica_groups=mesh['section'=4,'expert'=64] {'expert'}, dimensions={0} | all-to-all | bytes 1474560 | tf_op jit(solution)/shard_map/all_to_all | solution.py:78
  122.5 7.3 %fusion.8 = f32[256,2880]{0,1:T(8,128)S(1)} fusion(bf16[256,1440]{1,0:T(8,128)(2,1)S(1)} %reshape.267, bf16[1,1,1440,2880]{3,2,1,0:T(8,128)(2,1)} %param.8), kind=kOutput, calls=%fused_computation.8 | convolution fusion | flops 2123366400 | bytes 11980800 | tf_op jit(solution)/shard_map/dot_general | solution.py:18
  129.7 4.4 fusion.27
  135.5 6.2 %all-to-all-start.3 = ((bf16[64,4,1440]{2,1,0:T(4,128)(2,1)}), bf16[64,4,1440]{2,1,0:T(4,128)(2,1)S(1)}, u32[]{:S(2)}, u32[]{:S(2)}) async-start(bf16[64,4,1440]{2,1,0:T(4,128)(2,1)} %reshape.268), calls=%async_computation.3 | async-start | bytes 1572864 | tf_op jit(solution)/shard_map/all_to_all | solution.py:81
  141.9 22.7 %all-to-all-done.3 = bf16[64,4,1440]{2,1,0:T(4,128)(2,1)S(1)} async-done(((bf16[64,4,1440]{2,1,0:T(4,128)(2,1)}), bf16[64,4,1440]{2,1,0:T(4,128)(2,1)S(1)}, u32[]{:S(2)}, u32[]{:S(2)}) %all-to-all-start.3) | async-done | bytes 737312 | tf_op jit(solution)/shard_map/all_to_all | solution.py:81
  165.4 4.1 collective-permute-start.1
  173.5 29.6 %all_to_all.62 = bf16[64,4,1440]{2,1,0:T(4,128)(2,1)S(1)} all-to-all(bf16[64,4,1440]{2,1,0:T(4,128)(2,1)S(1)} %reshape.270), channel_id=1, replica_groups=mesh['section'=4,'expert'=64] {'expert'}, dimensions={0} | all-to-all | bytes 1474560 | tf_op jit(solution)/shard_map/all_to_all | solution.py:78
  203.4 7.3 %fusion.6 = f32[256,2880]{0,1:T(8,128)S(1)} fusion(bf16[256,1440]{1,0:T(8,128)(2,1)S(1)} %reshape.271, bf16[1,1,1440,2880]{3,2,1,0:T(8,128)(2,1)} %param.8), kind=kOutput, calls=%fused_computation.6 | convolution fusion | flops 2123366400 | bytes 11980800 | tf_op jit(solution)/shard_map/dot_general | solution.py:18
  210.7 4.4 fusion.30
  216.4 6.2 %all-to-all-start.5 = ((bf16[64,4,1440]{2,1,0:T(4,128)(2,1)}), bf16[64,4,1440]{2,1,0:T(4,128)(2,1)S(1)}, u32[]{:S(2)}, u32[]{:S(2)}) async-start(bf16[64,4,1440]{2,1,0:T(4,128)(2,1)} %reshape.272), calls=%async_computation.5 | async-start | bytes 1572864 | tf_op jit(solution)/shard_map/all_to_all | solution.py:81
  222.8 22.7 %all-to-all-done.5 = bf16[64,4,1440]{2,1,0:T(4,128)(2,1)S(1)} async-done(((bf16[64,4,1440]{2,1,0:T(4,128)(2,1)}), bf16[64,4,1440]{2,1,0:T(4,128)(2,1)S(1)}, u32[]{:S(2)}, u32[]{:S(2)}) %all-to-all-start.5) | async-done | bytes 737312 | tf_op jit(solution)/shard_map/all_to_all | solution.py:81
  246.3 4.1 collective-permute-start.2
  254.4 29.8 %all_to_all.63 = bf16[64,4,1440]{2,1,0:T(4,128)(2,1)S(1)} all-to-all(bf16[64,4,1440]{2,1,0:T(4,128)(2,1)S(1)} %reshape.274), channel_id=1, replica_groups=mesh['section'=4,'expert'=64] {'expert'}, dimensions={0} | all-to-all | bytes 1474560 | tf_op jit(solution)/shard_map/all_to_all | solution.py:78
  284.5 7.3 %fusion.4 = f32[256,2880]{0,1:T(8,128)S(1)} fusion(bf16[256,1440]{1,0:T(8,128)(2,1)S(1)} %reshape.275, bf16[1,1,1440,2880]{3,2,1,0:T(8,128)(2,1)} %param.8), kind=kOutput, calls=%fused_computation.4 | convolution fusion | flops 2123366400 | bytes 11980800 | tf_op jit(solution)/shard_map/dot_general | solution.py:18
  291.8 4.4 fusion.33
  297.5 6.2 %all-to-all-start.7 = ((bf16[64,4,1440]{2,1,0:T(4,128)(2,1)}), bf16[64,4,1440]{2,1,0:T(4,128)(2,1)S(1)}, u32[]{:S(2)}, u32[]{:S(2)}) async-start(bf16[64,4,1440]{2,1,0:T(4,128)(2,1)} %reshape.276), calls=%async_computation.7 | async-start | bytes 1572864 | tf_op jit(solution)/shard_map/all_to_all | solution.py:81
  303.9 22.7 %all-to-all-done.7 = bf16[64,4,1440]{2,1,0:T(4,128)(2,1)S(1)} async-done(((bf16[64,4,1440]{2,1,0:T(4,128)(2,1)}), bf16[64,4,1440]{2,1,0:T(4,128)(2,1)S(1)}, u32[]{:S(2)}, u32[]{:S(2)}) %all-to-all-start.7) | async-done | bytes 737312 | tf_op jit(solution)/shard_map/all_to_all | solution.py:81
  335.5 29.8 %all_to_all.64 = bf16[64,4,1440]{2,1,0:T(4,128)(2,1)S(1)} all-to-all(bf16[64,4,1440]{2,1,0:T(4,128)(2,1)S(1)} %reshape.278), channel_id=1, replica_groups=mesh['section'=4,'expert'=64] {'expert'}, dimensions={0} | all-to-all | bytes 1474560 | tf_op jit(solution)/shard_map/all_to_all | solution.py:78
  365.7 7.3 %fusion.2 = f32[256,2880]{0,1:T(8,128)S(1)} fusion(bf16[256,1440]{1,0:T(8,128)(2,1)S(1)} %reshape.279, bf16[1,1,1440,2880]{3,2,1,0:T(8,128)(2,1)} %param.8), kind=kOutput, calls=%fused_computation.2 | convolution fusion | flops 2123366400 | bytes 11980800 | tf_op jit(solution)/shard_map/dot_general | solution.py:18
  372.9 4.4 fusion.36
  378.7 6.2 %all-to-all-start.9 = ((bf16[64,4,1440]{2,1,0:T(4,128)(2,1)}), bf16[64,4,1440]{2,1,0:T(4,128)(2,1)S(1)}, u32[]{:S(2)}, u32[]{:S(2)}) async-start(bf16[64,4,1440]{2,1,0:T(4,128)(2,1)} %reshape.280), calls=%async_computation.9 | async-start | bytes 1572864 | tf_op jit(solution)/shard_map/all_to_all | solution.py:81
  385.0 22.7 %all-to-all-done.9 = bf16[64,4,1440]{2,1,0:T(4,128)(2,1)S(1)} async-done(((bf16[64,4,1440]{2,1,0:T(4,128)(2,1)}), bf16[64,4,1440]{2,1,0:T(4,128)(2,1)S(1)}, u32[]{:S(2)}, u32[]{:S(2)}) %all-to-all-start.9) | async-done | bytes 737312 | tf_op jit(solution)/shard_map/all_to_all | solution.py:81
  416.6 29.9 %all_to_all.65 = bf16[64,4,1440]{2,1,0:T(4,128)(2,1)S(1)} all-to-all(bf16[64,4,1440]{2,1,0:T(4,128)(2,1)S(1)} %reshape.282), channel_id=1, replica_groups=mesh['section'=4,'expert'=64] {'expert'}, dimensions={0} | all-to-all | bytes 1474560 | tf_op jit(solution)/shard_map/all_to_all | solution.py:78
  446.8 7.3 %fusion = f32[256,2880]{0,1:T(8,128)S(1)} fusion(bf16[256,1440]{1,0:T(8,128)(2,1)S(1)} %reshape.283, bf16[1,1,1440,2880]{3,2,1,0:T(8,128)(2,1)} %param.8), kind=kOutput, calls=%fused_computation | convolution fusion | flops 2123366400 | bytes 11980800 | tf_op jit(solution)/shard_map/dot_general | solution.py:18
  454.1 4.4 fusion.39
  459.8 6.2 %all-to-all-start.11 = ((bf16[64,4,1440]{2,1,0:T(4,128)(2,1)}), bf16[64,4,1440]{2,1,0:T(4,128)(2,1)S(1)}, u32[]{:S(2)}, u32[]{:S(2)}) async-start(bf16[64,4,1440]{2,1,0:T(4,128)(2,1)} %reshape.284), calls=%async_computation.11 | async-start | bytes 1572864 | tf_op jit(solution)/shard_map/all_to_all | solution.py:81
  466.2 22.7 %all-to-all-done.11 = bf16[64,4,1440]{2,1,0:T(4,128)(2,1)S(1)} async-done(((bf16[64,4,1440]{2,1,0:T(4,128)(2,1)}), bf16[64,4,1440]{2,1,0:T(4,128)(2,1)S(1)}, u32[]{:S(2)}, u32[]{:S(2)}) %all-to-all-start.11) | async-done | bytes 737312 | tf_op jit(solution)/shard_map/all_to_all | solution.py:81
  (129 shorter events, 53.7 us)
Async XLA Ops:
  54.4 7.3 %copy-start.2 = (s32[1,6,24,4]{2,3,1,0:T(4,128)S(1)}, s32[1,6,24,4]{2,3,1,0:T(4,128)}, u32[]{:S(2)}) copy-start(s32[1,6,24,4]{2,3,1,0:T(4,128)} %param.11) | copy-start | bytes 6916
  54.4 7.7 %copy-start.1 = (bf16[6,24,1440]{2,1,0:T(8,128)(2,1)S(1)}, bf16[6,24,1440]{2,1,0:T(8,128)(2,1)}, u32[]{:S(2)}) copy-start(bf16[6,24,1440]{2,1,0:T(8,128)(2,1)} %param.6) | copy-start | bytes 1244164
  55.5 29.2 %all-to-all-start.1 = ((bf16[64,4,1440]{2,1,0:T(4,128)(2,1)}), bf16[64,4,1440]{2,1,0:T(4,128)(2,1)S(1)}, u32[]{:S(2)}, u32[]{:S(2)}) async-start(bf16[64,4,1440]{2,1,0:T(4,128)(2,1)} %reshape.264), calls=%async_computation.1 | async-start | bytes 1572864 | tf_op jit(solution)/shard_map/all_to_all | solution.py:81
  85.5 5.9 %collective-permute-start = (bf16[48,1440]{1,0:T(8,128)(2,1)S(1)}, bf16[48,1440]{1,0:T(8,128)(2,1)S(1)}, u32[]{:S(2)}, u32[]{:S(2)}) collective-permute-start(bf16[48,1440]{1,0:T(8,128)(2,1)S(1)} %get-tuple-element.104), channel_id=1, source_target_pairs={{0,64},{64,128},{128,192},{1,65},{65,129},{129,193},{2,66},{66,130... | collective-permute-start | bytes 414728 | tf_op jit(solution)/shard_map/ppermute | solution.py:93
  135.5 29.2 %all-to-all-start.3 = ((bf16[64,4,1440]{2,1,0:T(4,128)(2,1)}), bf16[64,4,1440]{2,1,0:T(4,128)(2,1)S(1)}, u32[]{:S(2)}, u32[]{:S(2)}) async-start(bf16[64,4,1440]{2,1,0:T(4,128)(2,1)} %reshape.268), calls=%async_computation.3 | async-start | bytes 1572864 | tf_op jit(solution)/shard_map/all_to_all | solution.py:81
  165.4 6.9 %collective-permute-start.1 = (bf16[48,1440]{1,0:T(8,128)(2,1)S(1)}, bf16[48,1440]{1,0:T(8,128)(2,1)S(1)}, u32[]{:S(2)}, u32[]{:S(2)}) collective-permute-start(bf16[48,1440]{1,0:T(8,128)(2,1)S(1)} %get-tuple-element.20), channel_id=1, source_target_pairs={{0,64},{64,128},{128,192},{1,65},{65,129},{129,193},{2,66},{66,130... | collective-permute-start | bytes 414728 | tf_op jit(solution)/shard_map/ppermute | solution.py:93
  216.4 29.2 %all-to-all-start.5 = ((bf16[64,4,1440]{2,1,0:T(4,128)(2,1)}), bf16[64,4,1440]{2,1,0:T(4,128)(2,1)S(1)}, u32[]{:S(2)}, u32[]{:S(2)}) async-start(bf16[64,4,1440]{2,1,0:T(4,128)(2,1)} %reshape.272), calls=%async_computation.5 | async-start | bytes 1572864 | tf_op jit(solution)/shard_map/all_to_all | solution.py:81
  246.3 6.9 %collective-permute-start.2 = (bf16[48,1440]{1,0:T(8,128)(2,1)S(1)}, bf16[48,1440]{1,0:T(8,128)(2,1)S(1)}, u32[]{:S(2)}, u32[]{:S(2)}) collective-permute-start(bf16[48,1440]{1,0:T(8,128)(2,1)S(1)} %get-tuple-element.16), channel_id=1, source_target_pairs={{0,64},{64,128},{128,192},{1,65},{65,129},{129,193},{2,66},{66,130... | collective-permute-start | bytes 414728 | tf_op jit(solution)/shard_map/ppermute | solution.py:93
  297.5 29.1 %all-to-all-start.7 = ((bf16[64,4,1440]{2,1,0:T(4,128)(2,1)}), bf16[64,4,1440]{2,1,0:T(4,128)(2,1)S(1)}, u32[]{:S(2)}, u32[]{:S(2)}) async-start(bf16[64,4,1440]{2,1,0:T(4,128)(2,1)} %reshape.276), calls=%async_computation.7 | async-start | bytes 1572864 | tf_op jit(solution)/shard_map/all_to_all | solution.py:81
  327.4 6.9 %collective-permute-start.3 = (bf16[48,1440]{1,0:T(8,128)(2,1)S(1)}, bf16[48,1440]{1,0:T(8,128)(2,1)S(1)}, u32[]{:S(2)}, u32[]{:S(2)}) collective-permute-start(bf16[48,1440]{1,0:T(8,128)(2,1)S(1)} %get-tuple-element.12), channel_id=1, source_target_pairs={{0,64},{64,128},{128,192},{1,65},{65,129},{129,193},{2,66},{66,130... | collective-permute-start | bytes 414728 | tf_op jit(solution)/shard_map/ppermute | solution.py:93
  378.7 29.1 %all-to-all-start.9 = ((bf16[64,4,1440]{2,1,0:T(4,128)(2,1)}), bf16[64,4,1440]{2,1,0:T(4,128)(2,1)S(1)}, u32[]{:S(2)}, u32[]{:S(2)}) async-start(bf16[64,4,1440]{2,1,0:T(4,128)(2,1)} %reshape.280), calls=%async_computation.9 | async-start | bytes 1572864 | tf_op jit(solution)/shard_map/all_to_all | solution.py:81
  408.5 6.9 %collective-permute-start.4 = (bf16[48,1440]{1,0:T(8,128)(2,1)S(1)}, bf16[48,1440]{1,0:T(8,128)(2,1)S(1)}, u32[]{:S(2)}, u32[]{:S(2)}) collective-permute-start(bf16[48,1440]{1,0:T(8,128)(2,1)S(1)} %get-tuple-element.8), channel_id=1, source_target_pairs={{0,64},{64,128},{128,192},{1,65},{65,129},{129,193},{2,66},{66,130... | collective-permute-start | bytes 414728 | tf_op jit(solution)/shard_map/ppermute | solution.py:93
  459.8 29.1 %all-to-all-start.11 = ((bf16[64,4,1440]{2,1,0:T(4,128)(2,1)}), bf16[64,4,1440]{2,1,0:T(4,128)(2,1)S(1)}, u32[]{:S(2)}, u32[]{:S(2)}) async-start(bf16[64,4,1440]{2,1,0:T(4,128)(2,1)} %reshape.284), calls=%async_computation.11 | async-start | bytes 1572864 | tf_op jit(solution)/shard_map/all_to_all | solution.py:81
  489.7 0.8 copy-start

commit v2 on v1

--- a/solution.py
+++ b/solution.py
@@ -1,9 +1,13 @@
 import jax
 import jax.numpy as jnp
 from jax import lax
+from jax.experimental import pallas as pl
+from jax.experimental.pallas import tpu as pltpu
 from jax.sharding import PartitionSpec as P
 
 CHUNK = 2
+ROW_STEP = 32
+COLUMN_BLOCKS = ((0, 1024), (1024, 1920), (1920, 2880))
 
 
 def split_three(value):
@@ -13,15 +17,65 @@
     return [part.astype(jnp.bfloat16) for part in (high, middle, low)]
 
 
-def expert_ffn(rows, gate_up_w, down_w):
+def ffn_kernel(x_ref, gate_up_ref, down_ref, out_ref, gate_up_here, down_here, projected, activated, sems):
+    experts_n, per_expert, width = x_ref.shape
+    slots = experts_n * per_expert
+    hidden_units = down_ref.shape[0]
+    arriving = []
+    for number, (first, last) in enumerate(COLUMN_BLOCKS):
+        part = pl.ds(first, last - first)
+        arriving.append(
+            pltpu.make_async_copy(
+                gate_up_ref.at[:, part], gate_up_here.at[:, part], sems.at[number]
+            )
+        )
+    down_copy = pltpu.make_async_copy(down_ref, down_here, sems.at[len(COLUMN_BLOCKS)])
+    for copy in arriving:
+        copy.start()
+    rows = x_ref[...].reshape(slots, width)
+    for number, (first, last) in enumerate(COLUMN_BLOCKS):
+        arriving[number].wait()
+        if number == 0:
+            down_copy.start()
+        projected[:, first:last] = jnp.dot(
+            rows, gate_up_here[:, first:last], preferred_element_type=jnp.float32
+        )
+    for first in range(0, slots, ROW_STEP):
+        part = slice(first, first + ROW_STEP)
+        gate_part = projected[part, :hidden_units]
+        up_part = projected[part, hidden_units:]
+        activated[part, :] = (
+            gate_part * jax.nn.sigmoid(1.702 * gate_part) * (up_part + 1.0)
+        ).astype(jnp.bfloat16)
+    down_copy.wait()
+    result = jnp.dot(activated[...], down_here[...], preferred_element_type=jnp.float32)
+    out_ref[...] = result.reshape(experts_n, per_expert, width).astype(jnp.bfloat16)
+
+
+def expert_ffn(arrived, gate_up_w, down_w):
+    experts_n, per_expert, width = arrived.shape
+    slots = experts_n * per_expert
     hidden_units = down_w.shape[0]
-    projected = jnp.dot(rows, gate_up_w, preferred_element_type=jnp.float32)
-    gate_part = projected[:, :hidden_units]
-    up_part = projected[:, hidden_units:]
-    activated = (gate_part * jax.nn.sigmoid(1.702 * gate_part) * (up_part + 1.0)).astype(
-        jnp.bfloat16
+    whole = pl.BlockSpec(memory_space=pltpu.VMEM)
+    outside = pl.BlockSpec(memory_space=pltpu.HBM)
+    return pl.pallas_call(
+        ffn_kernel,
+        out_shape=jax.ShapeDtypeStruct(arrived.shape, arrived.dtype),
+        in_specs=[whole, outside, outside],
+        out_specs=whole,
+        scratch_shapes=[
+            pltpu.VMEM(gate_up_w.shape, gate_up_w.dtype),
+            pltpu.VMEM(down_w.shape, down_w.dtype),
+            pltpu.VMEM((slots, 2 * hidden_units), jnp.float32),
+            pltpu.VMEM((slots, hidden_units), jnp.bfloat16),
+            pltpu.SemaphoreType.DMA((len(COLUMN_BLOCKS) + 1,)),
+        ],
+        compiler_params=pltpu.CompilerParams(vmem_limit_bytes=40 << 20),
+    )(
+        arrived,
+        pltpu.with_memory_space_constraint(gate_up_w, pltpu.HBM),
+        pltpu.with_memory_space_constraint(down_w, pltpu.HBM),
     )
-    return jnp.dot(activated, down_w, preferred_element_type=jnp.float32).astype(jnp.bfloat16)
 
 
 def shards(tokens, norm_gain, gate_up, down, routes, route_weights):
@@ -50,18 +104,13 @@
     shares = shares.reshape(chunk_count, rows_n, chosen)
     chunks = tokens.reshape(chunk_count, rows_n, width)
 
-    incoming = jnp.zeros((rows_n, width), jnp.bfloat16)
-    results = jnp.zeros((chunk_count, rows_n, width), jnp.bfloat16)
-    tick_total = chunk_count + sections - 1
-    for tick_number in range(tick_total):
-        fresh_input = chunks[min(tick_number, chunk_count - 1)]
-        stream = jnp.where(section_index == 0, fresh_input, incoming)
+    slot_ids = jnp.arange(slots, dtype=jnp.int32)
+
+    def step(tick_number, stream, results):
         chunk_here = tick_number - section_index
         clamped = jnp.clip(chunk_here, 0, chunk_count - 1)
         target_rows = lax.dynamic_index_in_dim(target, clamped, 0, keepdims=False)
         share_rows = lax.dynamic_index_in_dim(shares, clamped, 0, keepdims=False)
-
-        slot_ids = jnp.arange(slots, dtype=jnp.int32)
         hits = [slot_ids[:, None] == target_rows[None, :, k] for k in range(chosen)]
         placing = sum(h.astype(jnp.float32) for h in hits).astype(jnp.bfloat16)
         mixing = sum(
@@ -76,8 +125,7 @@
         outgoing = jnp.dot(placing, normed, preferred_element_type=jnp.float32).astype(jnp.bfloat16)
         outgoing = outgoing.reshape(experts_n, per_expert, width)
         arrived = lax.all_to_all(outgoing, "expert", split_axis=0, concat_axis=0, tiled=True)
-        computed = expert_ffn(arrived.reshape(slots, width), gate_up_w, down_w)
-        computed = computed.reshape(experts_n, per_expert, width)
+        computed = expert_ffn(arrived, gate_up_w, down_w)
         returned = lax.all_to_all(computed, "expert", split_axis=0, concat_axis=0, tiled=True)
         returned_rows = returned.reshape(slots, width)
         mixed = jnp.dot(mixing, returned_rows, preferred_element_type=jnp.float32)
@@ -89,11 +137,21 @@
         results = lax.dynamic_update_index_in_dim(
             results, jnp.where(active, output_rows, kept), clamped, 0
         )
-        if tick_number + 1 < tick_total:
-            incoming = lax.ppermute(
-                output_rows, "section", [(s, s + 1) for s in range(sections - 1)]
-            )
-    return results.reshape(1, micro_count, token_count, width)
+        return output_rows, results
+
+    def relayed(tick_number, carried):
+        previous, results = carried
+        incoming = lax.ppermute(previous, "section", [(s, (s + 1) % sections) for s in range(sections)])
+        fresh_input = lax.dynamic_index_in_dim(
+            chunks, jnp.minimum(tick_number, chunk_count - 1), 0, keepdims=False
+        )
+        return step(tick_number, jnp.where(section_index == 0, fresh_input, incoming), results)
+
+    results = jnp.zeros((chunk_count, rows_n, width), jnp.bfloat16)
+    first_stream = jnp.where(section_index == 0, chunks[0], jnp.zeros_like(chunks[0]))
+    carried = step(0, first_stream, results)
+    carried = lax.fori_loop(1, chunk_count + sections - 1, relayed, carried)
+    return carried[1].reshape(1, micro_count, token_count, width)
 
 
 def solution(mesh):

time: 500 us -> 453 us (0.906); the launches traced: 491 us -> 452 us
  matrix products: 74.3 us -> 4.48 us
  Pallas kernels: 0 us -> 44 us
  starting transfers between devices: 57 us -> 39.2 us
  waiting for transfers between devices: 150 us -> 166 us
  local copies, waits for them, and re-layouts: 17.9 us -> 7.65 us
    dot_general x24 -> x12, matrix products: 74.3 us -> 4.48 us  [the longest x6 2.79 us: step(): jnp.dot(placing, normed, preferred_element_type=jnp.float32)]
    pallas_call x0 -> x6, Pallas kernels: none -> 44 us  [expert_ffn(): pl.pallas_call(ffn_kernel, out_shape=jax.ShapeDtypeStruct(arrived.shape,...]
    ppermute x5, starting transfers between devices: 19.8 us -> 1.63 us  [relayed(): lax.ppermute(previous, 'section', [(s, (s + 1) % sections) for s in range...]
    ppermute x5, waiting for transfers between devices: 13.6 us -> 29.5 us  [relayed(): lax.ppermute(previous, 'section', [(s, (s + 1) % sections) for s in range...]
    reshape x24 -> x12, local copies, waits for them, and re-layouts: 12 us -> 3.34 us  [the longest x6 2.2 us: step(): returned_rows = returned.reshape(slots, width)]
where the time goes in v2:
time: 453 us; the launch traced here: 452 us
  blocking collectives  184 us (41%)
  waiting for transfers between devices  166 us (37%)
  Pallas kernels  44 us (10%)
  starting transfers between devices  39.2 us (9%)
  local copies, waits for them, and re-layouts  7.65 us (2%)
  other arithmetic  6.05 us (1%)
    all_to_all x6, blocking collectives, step(): lax.all_to_all(outgoing, 'expert', split_axis=0, concat_axis=0, tiled=True)  184 us
    all_to_all x6, waiting for transfers between devices, step(): lax.all_to_all(computed, 'expert', split_axis=0, concat_axis=0, tiled=True)  136 us
    pallas_call x6, Pallas kernels, expert_ffn(): pl.pallas_call(ffn_kernel, out_shape=jax.ShapeDtypeStruct(arrived.shape,...  44 us
    all_to_all x6, starting transfers between devices, step(): lax.all_to_all(computed, 'expert', split_axis=0, concat_axis=0, tiled=True)  37.5 us
    ppermute x5, waiting for transfers between devices, relayed(): lax.ppermute(previous, 'section', [(s, (s + 1) % sections) for s in range...  29.5 us
  transfers between devices with their start and end apart: 11, of which 11 were waited for; matrix products, arithmetic and copies ran while one was open for 0% of the time, Pallas kernels for 0%

profile of v2, /device:TPU:1, one launch (start us, length us, event | category | flops | bytes accessed | tf_op | source)
XLA Modules:
  0.0 451.7 jit_solution(15937593213227741535)
XLA Ops:
  2.4 1.0 fusion.25
  6.2 35.9 %all_to_all.31.x_ref = bf16[64,4,1440]{2,1,0:T(4,128)(2,1)S(1)} all-to-all(bf16[64,4,1440]{2,1,0:T(4,128)(2,1)S(1)} %reshape.141), channel_id=1, replica_groups=mesh['section'=4,'expert'=64] {'expert'}, dimensions={0} | all-to-all | bytes 1474560 | tf_op jit(solution)/shard_map/all_to_all | solution.py:127
  42.1 7.3 %shard_map.64 = bf16[64,4,1440]{2,1,0:T(4,128)(2,1)} custom-call(bf16[64,4,1440]{2,1,0:T(4,128)(2,1)S(1)} %all_to_all.31.x_ref, bf16[1440,2880]{1,0:T(8,128)(2,1)} %bitcast.85, bf16[1440,1440]{1,0:T(8,128)(2,1)} %bitcast.87), custom_call_target="tpu_custom_call" | custom-call | tf_op jit(solution)/shard_map/pallas_call | solution.py:61
  49.4 6.4 %all-to-all-start.3 = ((bf16[64,4,1440]{2,1,0:T(4,128)(2,1)}), bf16[64,4,1440]{2,1,0:T(4,128)(2,1)S(1)}, u32[]{:S(2)}, u32[]{:S(2)}) async-start(bf16[64,4,1440]{2,1,0:T(4,128)(2,1)} %shard_map.64), calls=%async_computation.3 | async-start | bytes 1572864 | tf_op jit(solution)/shard_map/all_to_all | solution.py:129
  56.2 22.5 %all-to-all-done.3 = bf16[64,4,1440]{2,1,0:T(4,128)(2,1)S(1)} async-done(((bf16[64,4,1440]{2,1,0:T(4,128)(2,1)}), bf16[64,4,1440]{2,1,0:T(4,128)(2,1)S(1)}, u32[]{:S(2)}, u32[]{:S(2)}) %all-to-all-start.3) | async-done | bytes 737312 | tf_op jit(solution)/shard_map/all_to_all | solution.py:129
  79.5 371.4 %while.18 = (s32[]{:T(128)}, bf16[48,1440]{1,0:T(8,128)(2,1)S(1)}, bf16[3,48,1440]{2,1,0:T(8,128)(2,1)S(1)}, pred[]{:T(512)}, bf16[3,48,1440]{2,1,0:T(8,128)(2,1...) while((s32[]{:T(128)}, bf16[48,1440]{1,0:T(8,128)(2,1)S(1)}, ...), condition=%wide.region_5.6_spmd.clone.clone, body=%wide.region_3.5_spmd.clone.clone.sunk | while | flops 143483968 | bytes 13543646 | solution.py:153
  79.5 1.3 collective-permute-start
  80.9 5.0 %collective-permute-done = bf16[48,1440]{1,0:T(8,128)(2,1)S(1)} collective-permute-done((bf16[48,1440]{1,0:T(8,128)(2,1)S(1)}, bf16[48,1440]{1,0:T(8,128)(2,1)S(1)}, u32[]{:S(2)}, u32[]{:S(2)}) %collective-permute-start) | collective-permute-done | bytes 138272 | tf_op jit(solution)/shard_map/while/body/eval_jaxpr/ppermute | solution.py:144
  87.0 29.6 %all_to_all.32.x_ref = bf16[64,4,1440]{2,1,0:T(4,128)(2,1)S(1)} all-to-all(bf16[64,4,1440]{2,1,0:T(4,128)(2,1)S(1)} %reshape.154), channel_id=1, replica_groups=mesh['section'=4,'expert'=64] {'expert'}, dimensions={0} | all-to-all | bytes 1474560 | tf_op jit(solution)/shard_map/while/body/eval_jaxpr/all_to_all | solution.py:127
  116.6 7.3 %eval_jaxpr.6 = bf16[64,4,1440]{2,1,0:T(4,128)(2,1)} custom-call(bf16[64,4,1440]{2,1,0:T(4,128)(2,1)S(1)} %all_to_all.32.x_ref, bf16[1440,2880]{1,0:T(8,128)(2,1)} %get-tuple-element.535.gate_up_ref, bf16[1440,1440]{1,0:T(8,128)(2,1)} %get-tuple-element.536.down_ref), custom_call_target="tpu_custom_call" | custom-call | tf_op jit(solution)/shard_map/while/body/eval_jaxpr/pallas_call | solution.py:61
  123.9 6.2 %all-to-all-start.1 = ((bf16[64,4,1440]{2,1,0:T(4,128)(2,1)}), bf16[64,4,1440]{2,1,0:T(4,128)(2,1)S(1)}, u32[]{:S(2)}, u32[]{:S(2)}) async-start(bf16[64,4,1440]{2,1,0:T(4,128)(2,1)} %eval_jaxpr.6), calls=%async_computation.1 | async-start | bytes 1572864 | tf_op jit(solution)/shard_map/while/body/eval_jaxpr/all_to_all | solution.py:129
  130.3 22.7 %all-to-all-done.1 = bf16[64,4,1440]{2,1,0:T(4,128)(2,1)S(1)} async-done(((bf16[64,4,1440]{2,1,0:T(4,128)(2,1)}), bf16[64,4,1440]{2,1,0:T(4,128)(2,1)S(1)}, u32[]{:S(2)}, u32[]{:S(2)}) %all-to-all-start.1) | async-done | bytes 737312 | tf_op jit(solution)/shard_map/while/body/eval_jaxpr/all_to_all | solution.py:129
  154.0 6.1 %collective-permute-done = bf16[48,1440]{1,0:T(8,128)(2,1)S(1)} collective-permute-done((bf16[48,1440]{1,0:T(8,128)(2,1)S(1)}, bf16[48,1440]{1,0:T(8,128)(2,1)S(1)}, u32[]{:S(2)}, u32[]{:S(2)}) %collective-permute-start) | collective-permute-done | bytes 138272 | tf_op jit(solution)/shard_map/while/body/eval_jaxpr/ppermute | solution.py:144
  161.2 29.6 %all_to_all.32.x_ref = bf16[64,4,1440]{2,1,0:T(4,128)(2,1)S(1)} all-to-all(bf16[64,4,1440]{2,1,0:T(4,128)(2,1)S(1)} %reshape.154), channel_id=1, replica_groups=mesh['section'=4,'expert'=64] {'expert'}, dimensions={0} | all-to-all | bytes 1474560 | tf_op jit(solution)/shard_map/while/body/eval_jaxpr/all_to_all | solution.py:127
  190.8 7.3 %eval_jaxpr.6 = bf16[64,4,1440]{2,1,0:T(4,128)(2,1)} custom-call(bf16[64,4,1440]{2,1,0:T(4,128)(2,1)S(1)} %all_to_all.32.x_ref, bf16[1440,2880]{1,0:T(8,128)(2,1)} %get-tuple-element.535.gate_up_ref, bf16[1440,1440]{1,0:T(8,128)(2,1)} %get-tuple-element.536.down_ref), custom_call_target="tpu_custom_call" | custom-call | tf_op jit(solution)/shard_map/while/body/eval_jaxpr/pallas_call | solution.py:61
  198.2 6.2 %all-to-all-start.1 = ((bf16[64,4,1440]{2,1,0:T(4,128)(2,1)}), bf16[64,4,1440]{2,1,0:T(4,128)(2,1)S(1)}, u32[]{:S(2)}, u32[]{:S(2)}) async-start(bf16[64,4,1440]{2,1,0:T(4,128)(2,1)} %eval_jaxpr.6), calls=%async_computation.1 | async-start | bytes 1572864 | tf_op jit(solution)/shard_map/while/body/eval_jaxpr/all_to_all | solution.py:129
  204.6 22.7 %all-to-all-done.1 = bf16[64,4,1440]{2,1,0:T(4,128)(2,1)S(1)} async-done(((bf16[64,4,1440]{2,1,0:T(4,128)(2,1)}), bf16[64,4,1440]{2,1,0:T(4,128)(2,1)S(1)}, u32[]{:S(2)}, u32[]{:S(2)}) %all-to-all-start.1) | async-done | bytes 737312 | tf_op jit(solution)/shard_map/while/body/eval_jaxpr/all_to_all | solution.py:129
  228.3 6.1 %collective-permute-done = bf16[48,1440]{1,0:T(8,128)(2,1)S(1)} collective-permute-done((bf16[48,1440]{1,0:T(8,128)(2,1)S(1)}, bf16[48,1440]{1,0:T(8,128)(2,1)S(1)}, u32[]{:S(2)}, u32[]{:S(2)}) %collective-permute-start) | collective-permute-done | bytes 138272 | tf_op jit(solution)/shard_map/while/body/eval_jaxpr/ppermute | solution.py:144
  235.5 29.6 %all_to_all.32.x_ref = bf16[64,4,1440]{2,1,0:T(4,128)(2,1)S(1)} all-to-all(bf16[64,4,1440]{2,1,0:T(4,128)(2,1)S(1)} %reshape.154), channel_id=1, replica_groups=mesh['section'=4,'expert'=64] {'expert'}, dimensions={0} | all-to-all | bytes 1474560 | tf_op jit(solution)/shard_map/while/body/eval_jaxpr/all_to_all | solution.py:127
  265.1 7.3 %eval_jaxpr.6 = bf16[64,4,1440]{2,1,0:T(4,128)(2,1)} custom-call(bf16[64,4,1440]{2,1,0:T(4,128)(2,1)S(1)} %all_to_all.32.x_ref, bf16[1440,2880]{1,0:T(8,128)(2,1)} %get-tuple-element.535.gate_up_ref, bf16[1440,1440]{1,0:T(8,128)(2,1)} %get-tuple-element.536.down_ref), custom_call_target="tpu_custom_call" | custom-call | tf_op jit(solution)/shard_map/while/body/eval_jaxpr/pallas_call | solution.py:61
  272.4 6.2 %all-to-all-start.1 = ((bf16[64,4,1440]{2,1,0:T(4,128)(2,1)}), bf16[64,4,1440]{2,1,0:T(4,128)(2,1)S(1)}, u32[]{:S(2)}, u32[]{:S(2)}) async-start(bf16[64,4,1440]{2,1,0:T(4,128)(2,1)} %eval_jaxpr.6), calls=%async_computation.1 | async-start | bytes 1572864 | tf_op jit(solution)/shard_map/while/body/eval_jaxpr/all_to_all | solution.py:129
  278.9 22.7 %all-to-all-done.1 = bf16[64,4,1440]{2,1,0:T(4,128)(2,1)S(1)} async-done(((bf16[64,4,1440]{2,1,0:T(4,128)(2,1)}), bf16[64,4,1440]{2,1,0:T(4,128)(2,1)S(1)}, u32[]{:S(2)}, u32[]{:S(2)}) %all-to-all-start.1) | async-done | bytes 737312 | tf_op jit(solution)/shard_map/while/body/eval_jaxpr/all_to_all | solution.py:129
  302.5 6.1 %collective-permute-done = bf16[48,1440]{1,0:T(8,128)(2,1)S(1)} collective-permute-done((bf16[48,1440]{1,0:T(8,128)(2,1)S(1)}, bf16[48,1440]{1,0:T(8,128)(2,1)S(1)}, u32[]{:S(2)}, u32[]{:S(2)}) %collective-permute-start) | collective-permute-done | bytes 138272 | tf_op jit(solution)/shard_map/while/body/eval_jaxpr/ppermute | solution.py:144
  309.8 29.6 %all_to_all.32.x_ref = bf16[64,4,1440]{2,1,0:T(4,128)(2,1)S(1)} all-to-all(bf16[64,4,1440]{2,1,0:T(4,128)(2,1)S(1)} %reshape.154), channel_id=1, replica_groups=mesh['section'=4,'expert'=64] {'expert'}, dimensions={0} | all-to-all | bytes 1474560 | tf_op jit(solution)/shard_map/while/body/eval_jaxpr/all_to_all | solution.py:127
  339.4 7.3 %eval_jaxpr.6 = bf16[64,4,1440]{2,1,0:T(4,128)(2,1)} custom-call(bf16[64,4,1440]{2,1,0:T(4,128)(2,1)S(1)} %all_to_all.32.x_ref, bf16[1440,2880]{1,0:T(8,128)(2,1)} %get-tuple-element.535.gate_up_ref, bf16[1440,1440]{1,0:T(8,128)(2,1)} %get-tuple-element.536.down_ref), custom_call_target="tpu_custom_call" | custom-call | tf_op jit(solution)/shard_map/while/body/eval_jaxpr/pallas_call | solution.py:61
  346.7 6.2 %all-to-all-start.1 = ((bf16[64,4,1440]{2,1,0:T(4,128)(2,1)}), bf16[64,4,1440]{2,1,0:T(4,128)(2,1)S(1)}, u32[]{:S(2)}, u32[]{:S(2)}) async-start(bf16[64,4,1440]{2,1,0:T(4,128)(2,1)} %eval_jaxpr.6), calls=%async_computation.1 | async-start | bytes 1572864 | tf_op jit(solution)/shard_map/while/body/eval_jaxpr/all_to_all | solution.py:129
  353.2 22.7 %all-to-all-done.1 = bf16[64,4,1440]{2,1,0:T(4,128)(2,1)S(1)} async-done(((bf16[64,4,1440]{2,1,0:T(4,128)(2,1)}), bf16[64,4,1440]{2,1,0:T(4,128)(2,1)S(1)}, u32[]{:S(2)}, u32[]{:S(2)}) %all-to-all-start.1) | async-done | bytes 737312 | tf_op jit(solution)/shard_map/while/body/eval_jaxpr/all_to_all | solution.py:129
  376.8 6.1 %collective-permute-done = bf16[48,1440]{1,0:T(8,128)(2,1)S(1)} collective-permute-done((bf16[48,1440]{1,0:T(8,128)(2,1)S(1)}, bf16[48,1440]{1,0:T(8,128)(2,1)S(1)}, u32[]{:S(2)}, u32[]{:S(2)}) %collective-permute-start) | collective-permute-done | bytes 138272 | tf_op jit(solution)/shard_map/while/body/eval_jaxpr/ppermute | solution.py:144
  384.1 29.6 %all_to_all.32.x_ref = bf16[64,4,1440]{2,1,0:T(4,128)(2,1)S(1)} all-to-all(bf16[64,4,1440]{2,1,0:T(4,128)(2,1)S(1)} %reshape.154), channel_id=1, replica_groups=mesh['section'=4,'expert'=64] {'expert'}, dimensions={0} | all-to-all | bytes 1474560 | tf_op jit(solution)/shard_map/while/body/eval_jaxpr/all_to_all | solution.py:127
  413.7 7.3 %eval_jaxpr.6 = bf16[64,4,1440]{2,1,0:T(4,128)(2,1)} custom-call(bf16[64,4,1440]{2,1,0:T(4,128)(2,1)S(1)} %all_to_all.32.x_ref, bf16[1440,2880]{1,0:T(8,128)(2,1)} %get-tuple-element.535.gate_up_ref, bf16[1440,1440]{1,0:T(8,128)(2,1)} %get-tuple-element.536.down_ref), custom_call_target="tpu_custom_call" | custom-call | tf_op jit(solution)/shard_map/while/body/eval_jaxpr/pallas_call | solution.py:61
  421.0 6.2 %all-to-all-start.1 = ((bf16[64,4,1440]{2,1,0:T(4,128)(2,1)}), bf16[64,4,1440]{2,1,0:T(4,128)(2,1)S(1)}, u32[]{:S(2)}, u32[]{:S(2)}) async-start(bf16[64,4,1440]{2,1,0:T(4,128)(2,1)} %eval_jaxpr.6), calls=%async_computation.1 | async-start | bytes 1572864 | tf_op jit(solution)/shard_map/while/body/eval_jaxpr/all_to_all | solution.py:129
  427.4 22.7 %all-to-all-done.1 = bf16[64,4,1440]{2,1,0:T(4,128)(2,1)S(1)} async-done(((bf16[64,4,1440]{2,1,0:T(4,128)(2,1)}), bf16[64,4,1440]{2,1,0:T(4,128)(2,1)S(1)}, u32[]{:S(2)}, u32[]{:S(2)}) %all-to-all-start.1) | async-done | bytes 737312 | tf_op jit(solution)/shard_map/while/body/eval_jaxpr/all_to_all | solution.py:129
  (122 shorter events, 17.5 us)
Async XLA Ops:
  42.0 13.8 %copy-start.3 = (s32[1,6,24,4]{2,3,1,0:T(4,128)S(1)}, s32[1,6,24,4]{2,3,1,0:T(4,128)}, u32[]{:S(2)}) copy-start(s32[1,6,24,4]{2,3,1,0:T(4,128)} %param.13) | copy-start | bytes 6916
  49.4 30.0 %copy-start.1 = (bf16[6,24,1440]{2,1,0:T(8,128)(2,1)S(1)}, bf16[6,24,1440]{2,1,0:T(8,128)(2,1)}, u32[]{:S(2)}) copy-start(bf16[6,24,1440]{2,1,0:T(8,128)(2,1)} %param.8) | copy-start | bytes 1244164
  49.4 30.1 %copy-start.2 = (f32[1,1440]{1,0:T(1,128)S(1)}, f32[1,1440]{1,0:T(1,128)}, u32[]{:S(2)}) copy-start(f32[1,1440]{1,0:T(1,128)} %param.9) | copy-start | bytes 17284
  49.4 29.3 %all-to-all-start.3 = ((bf16[64,4,1440]{2,1,0:T(4,128)(2,1)}), bf16[64,4,1440]{2,1,0:T(4,128)(2,1)S(1)}, u32[]{:S(2)}, u32[]{:S(2)}) async-start(bf16[64,4,1440]{2,1,0:T(4,128)(2,1)} %shard_map.64), calls=%async_computation.3 | async-start | bytes 1572864 | tf_op jit(solution)/shard_map/all_to_all | solution.py:129
  79.5 6.3 %collective-permute-start = (bf16[48,1440]{1,0:T(8,128)(2,1)S(1)}, bf16[48,1440]{1,0:T(8,128)(2,1)S(1)}, u32[]{:S(2)}, u32[]{:S(2)}) collective-permute-start(bf16[48,1440]{1,0:T(8,128)(2,1)S(1)} %get-tuple-element.511), channel_id=1, source_target_pairs={{0,64},{64,128},{128,192},{192,0},{1,65},{65,129},{129,193},{193,1... | collective-permute-start | bytes 414728 | tf_op jit(solution)/shard_map/while/body/eval_jaxpr/ppermute | solution.py:144
  123.9 29.2 %all-to-all-start.1 = ((bf16[64,4,1440]{2,1,0:T(4,128)(2,1)}), bf16[64,4,1440]{2,1,0:T(4,128)(2,1)S(1)}, u32[]{:S(2)}, u32[]{:S(2)}) async-start(bf16[64,4,1440]{2,1,0:T(4,128)(2,1)} %eval_jaxpr.6), calls=%async_computation.1 | async-start | bytes 1572864 | tf_op jit(solution)/shard_map/while/body/eval_jaxpr/all_to_all | solution.py:129
  153.8 6.3 %collective-permute-start = (bf16[48,1440]{1,0:T(8,128)(2,1)S(1)}, bf16[48,1440]{1,0:T(8,128)(2,1)S(1)}, u32[]{:S(2)}, u32[]{:S(2)}) collective-permute-start(bf16[48,1440]{1,0:T(8,128)(2,1)S(1)} %get-tuple-element.511), channel_id=1, source_target_pairs={{0,64},{64,128},{128,192},{192,0},{1,65},{65,129},{129,193},{193,1... | collective-permute-start | bytes 414728 | tf_op jit(solution)/shard_map/while/body/eval_jaxpr/ppermute | solution.py:144
  198.2 29.2 %all-to-all-start.1 = ((bf16[64,4,1440]{2,1,0:T(4,128)(2,1)}), bf16[64,4,1440]{2,1,0:T(4,128)(2,1)S(1)}, u32[]{:S(2)}, u32[]{:S(2)}) async-start(bf16[64,4,1440]{2,1,0:T(4,128)(2,1)} %eval_jaxpr.6), calls=%async_computation.1 | async-start | bytes 1572864 | tf_op jit(solution)/shard_map/while/body/eval_jaxpr/all_to_all | solution.py:129
  228.1 6.3 %collective-permute-start = (bf16[48,1440]{1,0:T(8,128)(2,1)S(1)}, bf16[48,1440]{1,0:T(8,128)(2,1)S(1)}, u32[]{:S(2)}, u32[]{:S(2)}) collective-permute-start(bf16[48,1440]{1,0:T(8,128)(2,1)S(1)} %get-tuple-element.511), channel_id=1, source_target_pairs={{0,64},{64,128},{128,192},{192,0},{1,65},{65,129},{129,193},{193,1... | collective-permute-start | bytes 414728 | tf_op jit(solution)/shard_map/while/body/eval_jaxpr/ppermute | solution.py:144
  272.4 29.2 %all-to-all-start.1 = ((bf16[64,4,1440]{2,1,0:T(4,128)(2,1)}), bf16[64,4,1440]{2,1,0:T(4,128)(2,1)S(1)}, u32[]{:S(2)}, u32[]{:S(2)}) async-start(bf16[64,4,1440]{2,1,0:T(4,128)(2,1)} %eval_jaxpr.6), calls=%async_computation.1 | async-start | bytes 1572864 | tf_op jit(solution)/shard_map/while/body/eval_jaxpr/all_to_all | solution.py:129
  302.4 6.3 %collective-permute-start = (bf16[48,1440]{1,0:T(8,128)(2,1)S(1)}, bf16[48,1440]{1,0:T(8,128)(2,1)S(1)}, u32[]{:S(2)}, u32[]{:S(2)}) collective-permute-start(bf16[48,1440]{1,0:T(8,128)(2,1)S(1)} %get-tuple-element.511), channel_id=1, source_target_pairs={{0,64},{64,128},{128,192},{192,0},{1,65},{65,129},{129,193},{193,1... | collective-permute-start | bytes 414728 | tf_op jit(solution)/shard_map/while/body/eval_jaxpr/ppermute | solution.py:144
  346.7 29.2 %all-to-all-start.1 = ((bf16[64,4,1440]{2,1,0:T(4,128)(2,1)}), bf16[64,4,1440]{2,1,0:T(4,128)(2,1)S(1)}, u32[]{:S(2)}, u32[]{:S(2)}) async-start(bf16[64,4,1440]{2,1,0:T(4,128)(2,1)} %eval_jaxpr.6), calls=%async_computation.1 | async-start | bytes 1572864 | tf_op jit(solution)/shard_map/while/body/eval_jaxpr/all_to_all | solution.py:129
  376.6 6.3 %collective-permute-start = (bf16[48,1440]{1,0:T(8,128)(2,1)S(1)}, bf16[48,1440]{1,0:T(8,128)(2,1)S(1)}, u32[]{:S(2)}, u32[]{:S(2)}) collective-permute-start(bf16[48,1440]{1,0:T(8,128)(2,1)S(1)} %get-tuple-element.511), channel_id=1, source_target_pairs={{0,64},{64,128},{128,192},{192,0},{1,65},{65,129},{129,193},{193,1... | collective-permute-start | bytes 414728 | tf_op jit(solution)/shard_map/while/body/eval_jaxpr/ppermute | solution.py:144
  421.0 29.2 %all-to-all-start.1 = ((bf16[64,4,1440]{2,1,0:T(4,128)(2,1)}), bf16[64,4,1440]{2,1,0:T(4,128)(2,1)S(1)}, u32[]{:S(2)}, u32[]{:S(2)}) async-start(bf16[64,4,1440]{2,1,0:T(4,128)(2,1)} %eval_jaxpr.6), calls=%async_computation.1 | async-start | bytes 1572864 | tf_op jit(solution)/shard_map/while/body/eval_jaxpr/all_to_all | solution.py:129
  450.9 0.8 copy-start

commit v3 on v2

--- a/solution.py
+++ b/solution.py
@@ -106,7 +106,7 @@
 
     slot_ids = jnp.arange(slots, dtype=jnp.int32)
 
-    def step(tick_number, stream, results):
+    def step(tick_number, stream, results, ahead):
         chunk_here = tick_number - section_index
         clamped = jnp.clip(chunk_here, 0, chunk_count - 1)
         target_rows = lax.dynamic_index_in_dim(target, clamped, 0, keepdims=False)
@@ -124,6 +124,13 @@
         normed = (widened * scale * gain_row[None, :]).astype(jnp.bfloat16)
         outgoing = jnp.dot(placing, normed, preferred_element_type=jnp.float32).astype(jnp.bfloat16)
         outgoing = outgoing.reshape(experts_n, per_expert, width)
+        active = jnp.logical_and(chunk_here >= 0, chunk_here < chunk_count)
+        kept = lax.dynamic_index_in_dim(results, clamped, 0, keepdims=False)
+        place = clamped.astype(jnp.uint32)
+        if ahead:
+            outgoing, mixing, kept, active, place = lax.optimization_barrier(
+                (outgoing, mixing, kept, active, place)
+            )
         arrived = lax.all_to_all(outgoing, "expert", split_axis=0, concat_axis=0, tiled=True)
         computed = expert_ffn(arrived, gate_up_w, down_w)
         returned = lax.all_to_all(computed, "expert", split_axis=0, concat_axis=0, tiled=True)
@@ -132,10 +139,10 @@
         mixed = mixed.reshape(3, rows_n, width)
         output_rows = (widened + (mixed[0] + (mixed[1] + mixed[2]))).astype(jnp.bfloat16)
 
-        active = jnp.logical_and(chunk_here >= 0, chunk_here < chunk_count)
-        kept = lax.dynamic_index_in_dim(results, clamped, 0, keepdims=False)
-        results = lax.dynamic_update_index_in_dim(
-            results, jnp.where(active, output_rows, kept), clamped, 0
+        results = lax.dynamic_update_slice(
+            results,
+            jnp.where(active, output_rows, kept)[None],
+            (place, jnp.uint32(0), jnp.uint32(0)),
         )
         return output_rows, results
 
@@ -145,11 +152,11 @@
         fresh_input = lax.dynamic_index_in_dim(
             chunks, jnp.minimum(tick_number, chunk_count - 1), 0, keepdims=False
         )
-        return step(tick_number, jnp.where(section_index == 0, fresh_input, incoming), results)
+        return step(tick_number, jnp.where(section_index == 0, fresh_input, incoming), results, True)
 
     results = jnp.zeros((chunk_count, rows_n, width), jnp.bfloat16)
     first_stream = jnp.where(section_index == 0, chunks[0], jnp.zeros_like(chunks[0]))
-    carried = step(0, first_stream, results)
+    carried = step(0, first_stream, results, False)
     carried = lax.fori_loop(1, chunk_count + sections - 1, relayed, carried)
     return carried[1].reshape(1, micro_count, token_count, width)
 

time: 453 us -> 447 us (0.987)
  blocking collectives: 184 us -> 329 us
  waiting for transfers between devices: 166 us -> 50.9 us
  starting transfers between devices: 39.2 us -> 8 us
    all_to_all x0 -> x5, blocking collectives: none -> 145 us  [step(): lax.all_to_all(computed, 'expert', split_axis=0, concat_axis=0, tiled=True)]
    all_to_all x6 -> x1, waiting for transfers between devices: 136 us -> 22.5 us  [step(): lax.all_to_all(computed, 'expert', split_axis=0, concat_axis=0, tiled=True)]
    all_to_all x6 -> x1, starting transfers between devices: 37.5 us -> 6.37 us  [step(): lax.all_to_all(computed, 'expert', split_axis=0, concat_axis=0, tiled=True)]
  transfers between devices with their start and end apart: 11 -> 6, of which waited for: 11 -> 6; matrix products, arithmetic and copies ran while one was open for 0% -> 0% of each run, Pallas kernels for 0% -> 0%
where the time goes in v3:
time: 447 us; the launch traced here: 446 us
  blocking collectives  329 us (74%)
  waiting for transfers between devices  50.9 us (11%)
  Pallas kernels  39.6 us (9%)
  starting transfers between devices  8 us (2%)
  local copies, waits for them, and re-layouts  7.66 us (2%)
  other arithmetic  6.08 us (1%)
  matrix products  4.49 us (1%)
    all_to_all x6, blocking collectives, step(): lax.all_to_all(outgoing, 'expert', split_axis=0, concat_axis=0, tiled=True)  184 us
    all_to_all x5, blocking collectives, step(): lax.all_to_all(computed, 'expert', split_axis=0, concat_axis=0, tiled=True)  145 us
    pallas_call x6, Pallas kernels, expert_ffn(): pl.pallas_call(ffn_kernel, out_shape=jax.ShapeDtypeStruct(arrived.shape,...  39.6 us
    ppermute x5, waiting for transfers between devices, relayed(): lax.ppermute(previous, 'section', [(s, (s + 1) % sections) for s in range...  28.4 us
    all_to_all x1, waiting for transfers between devices, step(): lax.all_to_all(computed, 'expert', split_axis=0, concat_axis=0, tiled=True)  22.5 us
  transfers between devices with their start and end apart: 6, of which 6 were waited for; matrix products, arithmetic and copies ran while one was open for 0% of the time, Pallas kernels for 0%

profile of v3, /device:TPU:1, one launch (start us, length us, event | category | flops | bytes accessed | tf_op | source)
XLA Modules:
  0.0 446.2 jit_solution(12855328294178633178)
XLA Ops:
  0.0 0.7 broadcast_multiply_fusion
  0.7 0.8 copy.27
  1.6 1.0 fusion.18
  3.6 0.7 reduce.3
  4.3 1.0 fusion.20
  6.2 35.9 %all_to_all.31.x_ref = bf16[64,4,1440]{2,1,0:T(4,128)(2,1)S(1)} all-to-all(bf16[64,4,1440]{2,1,0:T(4,128)(2,1)S(1)} %reshape.141), channel_id=1, replica_groups=mesh['section'=4,'expert'=64] {'expert'}, dimensions={0} | all-to-all | bytes 1474560 | tf_op jit(solution)/shard_map/all_to_all | solution.py:134
  42.0 7.3 %shard_map.64 = bf16[64,4,1440]{2,1,0:T(4,128)(2,1)} custom-call(bf16[64,4,1440]{2,1,0:T(4,128)(2,1)S(1)} %all_to_all.31.x_ref, bf16[1440,2880]{1,0:T(8,128)(2,1)} %bitcast.86, bf16[1440,1440]{1,0:T(8,128)(2,1)} %bitcast.88), custom_call_target="tpu_custom_call" | custom-call | tf_op jit(solution)/shard_map/pallas_call | solution.py:61
  49.4 6.4 %all-to-all-start.3 = ((bf16[64,4,1440]{2,1,0:T(4,128)(2,1)}), bf16[64,4,1440]{2,1,0:T(4,128)(2,1)S(1)}, u32[]{:S(2)}, u32[]{:S(2)}) async-start(bf16[64,4,1440]{2,1,0:T(4,128)(2,1)} %shard_map.64), calls=%async_computation.3 | async-start | bytes 1572864 | tf_op jit(solution)/shard_map/all_to_all | solution.py:136
  56.2 22.5 %all-to-all-done.3 = bf16[64,4,1440]{2,1,0:T(4,128)(2,1)S(1)} async-done(((bf16[64,4,1440]{2,1,0:T(4,128)(2,1)}), bf16[64,4,1440]{2,1,0:T(4,128)(2,1)S(1)}, u32[]{:S(2)}, u32[]{:S(2)}) %all-to-all-start.3) | async-done | bytes 737312 | tf_op jit(solution)/shard_map/all_to_all | solution.py:136
  79.5 365.9 %while.18 = (s32[]{:T(128)}, bf16[48,1440]{1,0:T(8,128)(2,1)S(1)}, bf16[3,48,1440]{2,1,0:T(8,128)(2,1)S(1)}, pred[]{:T(512)}, bf16[3,48,1440]{2,1,0:T(8,128)(2,1...) while((s32[]{:T(128)}, bf16[48,1440]{1,0:T(8,128)(2,1)S(1)}, ...), condition=%wide.region_5.6_spmd.clone.clone, body=%wide.region_3.5_spmd.clone.clone.sunk | while | flops 143483968 | bytes 12855494 | solution.py:160
  79.5 1.3 collective-permute-start
  81.1 4.7 %collective-permute-done = bf16[48,1440]{1,0:T(8,128)(2,1)S(1)} collective-permute-done((bf16[48,1440]{1,0:T(8,128)(2,1)S(1)}, bf16[48,1440]{1,0:T(8,128)(2,1)S(1)}, u32[]{:S(2)}, u32[]{:S(2)}) %collective-permute-start) | collective-permute-done | bytes 138272 | tf_op jit(solution)/shard_map/while/body/eval_jaxpr/ppermute | solution.py:151
  87.0 29.6 %all_to_all.32.x_ref = bf16[64,4,1440]{2,1,0:T(4,128)(2,1)S(1)} all-to-all(bf16[64,4,1440]{2,1,0:T(4,128)(2,1)S(1)} %reshape.154), channel_id=1, replica_groups=mesh['section'=4,'expert'=64] {'expert'}, dimensions={0} | all-to-all | bytes 1474560 | tf_op jit(solution)/shard_map/while/body/eval_jaxpr/all_to_all | solution.py:134
  116.5 6.4 %eval_jaxpr.6 = bf16[64,4,1440]{2,1,0:T(4,128)(2,1)S(1)} custom-call(bf16[64,4,1440]{2,1,0:T(4,128)(2,1)S(1)} %all_to_all.32.x_ref, bf16[1440,2880]{1,0:T(8,128)(2,1)} %get-tuple-element.560.gate_up_ref, bf16[1440,1440]{1,0:T(8,128)(2,1)} %get-tuple-element.561.down_ref), custom_call_target="tpu_custom_call" | custom-call | tf_op jit(solution)/shard_map/while/body/eval_jaxpr/pallas_call | solution.py:61
  123.0 28.9 %all_to_all.33 = bf16[64,4,1440]{2,1,0:T(4,128)(2,1)S(1)} all-to-all(bf16[64,4,1440]{2,1,0:T(4,128)(2,1)S(1)} %eval_jaxpr.6), channel_id=1, replica_groups=mesh['section'=4,'expert'=64] {'expert'}, dimensions={0} | all-to-all | bytes 1474560 | tf_op jit(solution)/shard_map/while/body/eval_jaxpr/all_to_all | solution.py:136
  153.1 5.9 %collective-permute-done = bf16[48,1440]{1,0:T(8,128)(2,1)S(1)} collective-permute-done((bf16[48,1440]{1,0:T(8,128)(2,1)S(1)}, bf16[48,1440]{1,0:T(8,128)(2,1)S(1)}, u32[]{:S(2)}, u32[]{:S(2)}) %collective-permute-start) | collective-permute-done | bytes 138272 | tf_op jit(solution)/shard_map/while/body/eval_jaxpr/ppermute | solution.py:151
  160.1 29.6 %all_to_all.32.x_ref = bf16[64,4,1440]{2,1,0:T(4,128)(2,1)S(1)} all-to-all(bf16[64,4,1440]{2,1,0:T(4,128)(2,1)S(1)} %reshape.154), channel_id=1, replica_groups=mesh['section'=4,'expert'=64] {'expert'}, dimensions={0} | all-to-all | bytes 1474560 | tf_op jit(solution)/shard_map/while/body/eval_jaxpr/all_to_all | solution.py:134
  189.7 6.4 %eval_jaxpr.6 = bf16[64,4,1440]{2,1,0:T(4,128)(2,1)S(1)} custom-call(bf16[64,4,1440]{2,1,0:T(4,128)(2,1)S(1)} %all_to_all.32.x_ref, bf16[1440,2880]{1,0:T(8,128)(2,1)} %get-tuple-element.560.gate_up_ref, bf16[1440,1440]{1,0:T(8,128)(2,1)} %get-tuple-element.561.down_ref), custom_call_target="tpu_custom_call" | custom-call | tf_op jit(solution)/shard_map/while/body/eval_jaxpr/pallas_call | solution.py:61
  196.2 28.9 %all_to_all.33 = bf16[64,4,1440]{2,1,0:T(4,128)(2,1)S(1)} all-to-all(bf16[64,4,1440]{2,1,0:T(4,128)(2,1)S(1)} %eval_jaxpr.6), channel_id=1, replica_groups=mesh['section'=4,'expert'=64] {'expert'}, dimensions={0} | all-to-all | bytes 1474560 | tf_op jit(solution)/shard_map/while/body/eval_jaxpr/all_to_all | solution.py:136
  226.3 5.9 %collective-permute-done = bf16[48,1440]{1,0:T(8,128)(2,1)S(1)} collective-permute-done((bf16[48,1440]{1,0:T(8,128)(2,1)S(1)}, bf16[48,1440]{1,0:T(8,128)(2,1)S(1)}, u32[]{:S(2)}, u32[]{:S(2)}) %collective-permute-start) | collective-permute-done | bytes 138272 | tf_op jit(solution)/shard_map/while/body/eval_jaxpr/ppermute | solution.py:151
  233.3 29.6 %all_to_all.32.x_ref = bf16[64,4,1440]{2,1,0:T(4,128)(2,1)S(1)} all-to-all(bf16[64,4,1440]{2,1,0:T(4,128)(2,1)S(1)} %reshape.154), channel_id=1, replica_groups=mesh['section'=4,'expert'=64] {'expert'}, dimensions={0} | all-to-all | bytes 1474560 | tf_op jit(solution)/shard_map/while/body/eval_jaxpr/all_to_all | solution.py:134
  262.9 6.4 %eval_jaxpr.6 = bf16[64,4,1440]{2,1,0:T(4,128)(2,1)S(1)} custom-call(bf16[64,4,1440]{2,1,0:T(4,128)(2,1)S(1)} %all_to_all.32.x_ref, bf16[1440,2880]{1,0:T(8,128)(2,1)} %get-tuple-element.560.gate_up_ref, bf16[1440,1440]{1,0:T(8,128)(2,1)} %get-tuple-element.561.down_ref), custom_call_target="tpu_custom_call" | custom-call | tf_op jit(solution)/shard_map/while/body/eval_jaxpr/pallas_call | solution.py:61
  269.4 28.9 %all_to_all.33 = bf16[64,4,1440]{2,1,0:T(4,128)(2,1)S(1)} all-to-all(bf16[64,4,1440]{2,1,0:T(4,128)(2,1)S(1)} %eval_jaxpr.6), channel_id=1, replica_groups=mesh['section'=4,'expert'=64] {'expert'}, dimensions={0} | all-to-all | bytes 1474560 | tf_op jit(solution)/shard_map/while/body/eval_jaxpr/all_to_all | solution.py:136
  299.5 5.9 %collective-permute-done = bf16[48,1440]{1,0:T(8,128)(2,1)S(1)} collective-permute-done((bf16[48,1440]{1,0:T(8,128)(2,1)S(1)}, bf16[48,1440]{1,0:T(8,128)(2,1)S(1)}, u32[]{:S(2)}, u32[]{:S(2)}) %collective-permute-start) | collective-permute-done | bytes 138272 | tf_op jit(solution)/shard_map/while/body/eval_jaxpr/ppermute | solution.py:151
  306.5 29.6 %all_to_all.32.x_ref = bf16[64,4,1440]{2,1,0:T(4,128)(2,1)S(1)} all-to-all(bf16[64,4,1440]{2,1,0:T(4,128)(2,1)S(1)} %reshape.154), channel_id=1, replica_groups=mesh['section'=4,'expert'=64] {'expert'}, dimensions={0} | all-to-all | bytes 1474560 | tf_op jit(solution)/shard_map/while/body/eval_jaxpr/all_to_all | solution.py:134
  336.1 6.4 %eval_jaxpr.6 = bf16[64,4,1440]{2,1,0:T(4,128)(2,1)S(1)} custom-call(bf16[64,4,1440]{2,1,0:T(4,128)(2,1)S(1)} %all_to_all.32.x_ref, bf16[1440,2880]{1,0:T(8,128)(2,1)} %get-tuple-element.560.gate_up_ref, bf16[1440,1440]{1,0:T(8,128)(2,1)} %get-tuple-element.561.down_ref), custom_call_target="tpu_custom_call" | custom-call | tf_op jit(solution)/shard_map/while/body/eval_jaxpr/pallas_call | solution.py:61
  342.5 28.9 %all_to_all.33 = bf16[64,4,1440]{2,1,0:T(4,128)(2,1)S(1)} all-to-all(bf16[64,4,1440]{2,1,0:T(4,128)(2,1)S(1)} %eval_jaxpr.6), channel_id=1, replica_groups=mesh['section'=4,'expert'=64] {'expert'}, dimensions={0} | all-to-all | bytes 1474560 | tf_op jit(solution)/shard_map/while/body/eval_jaxpr/all_to_all | solution.py:136
  372.6 5.9 %collective-permute-done = bf16[48,1440]{1,0:T(8,128)(2,1)S(1)} collective-permute-done((bf16[48,1440]{1,0:T(8,128)(2,1)S(1)}, bf16[48,1440]{1,0:T(8,128)(2,1)S(1)}, u32[]{:S(2)}, u32[]{:S(2)}) %collective-permute-start) | collective-permute-done | bytes 138272 | tf_op jit(solution)/shard_map/while/body/eval_jaxpr/ppermute | solution.py:151
  379.7 29.6 %all_to_all.32.x_ref = bf16[64,4,1440]{2,1,0:T(4,128)(2,1)S(1)} all-to-all(bf16[64,4,1440]{2,1,0:T(4,128)(2,1)S(1)} %reshape.154), channel_id=1, replica_groups=mesh['section'=4,'expert'=64] {'expert'}, dimensions={0} | all-to-all | bytes 1474560 | tf_op jit(solution)/shard_map/while/body/eval_jaxpr/all_to_all | solution.py:134
  409.3 6.4 %eval_jaxpr.6 = bf16[64,4,1440]{2,1,0:T(4,128)(2,1)S(1)} custom-call(bf16[64,4,1440]{2,1,0:T(4,128)(2,1)S(1)} %all_to_all.32.x_ref, bf16[1440,2880]{1,0:T(8,128)(2,1)} %get-tuple-element.560.gate_up_ref, bf16[1440,1440]{1,0:T(8,128)(2,1)} %get-tuple-element.561.down_ref), custom_call_target="tpu_custom_call" | custom-call | tf_op jit(solution)/shard_map/while/body/eval_jaxpr/pallas_call | solution.py:61
  415.7 28.9 %all_to_all.33 = bf16[64,4,1440]{2,1,0:T(4,128)(2,1)S(1)} all-to-all(bf16[64,4,1440]{2,1,0:T(4,128)(2,1)S(1)} %eval_jaxpr.6), channel_id=1, replica_groups=mesh['section'=4,'expert'=64] {'expert'}, dimensions={0} | all-to-all | bytes 1474560 | tf_op jit(solution)/shard_map/while/body/eval_jaxpr/all_to_all | solution.py:136
  445.4 0.8 copy-done
  (122 shorter events, 13.5 us)
Async XLA Ops:
  42.0 13.8 %copy-start.3 = (s32[1,6,24,4]{2,3,1,0:T(4,128)S(1)}, s32[1,6,24,4]{2,3,1,0:T(4,128)}, u32[]{:S(2)}) copy-start(s32[1,6,24,4]{2,3,1,0:T(4,128)} %param.13) | copy-start | bytes 6916
  49.4 30.0 %copy-start.1 = (bf16[6,24,1440]{2,1,0:T(8,128)(2,1)S(1)}, bf16[6,24,1440]{2,1,0:T(8,128)(2,1)}, u32[]{:S(2)}) copy-start(bf16[6,24,1440]{2,1,0:T(8,128)(2,1)} %param.8) | copy-start | bytes 1244164
  49.4 30.1 %copy-start.2 = (f32[1,1440]{1,0:T(1,128)S(1)}, f32[1,1440]{1,0:T(1,128)}, u32[]{:S(2)}) copy-start(f32[1,1440]{1,0:T(1,128)} %param.9) | copy-start | bytes 17284
  49.4 29.3 %all-to-all-start.3 = ((bf16[64,4,1440]{2,1,0:T(4,128)(2,1)}), bf16[64,4,1440]{2,1,0:T(4,128)(2,1)S(1)}, u32[]{:S(2)}, u32[]{:S(2)}) async-start(bf16[64,4,1440]{2,1,0:T(4,128)(2,1)} %shard_map.64), calls=%async_computation.3 | async-start | bytes 1572864 | tf_op jit(solution)/shard_map/all_to_all | solution.py:136
  79.5 6.3 %collective-permute-start = (bf16[48,1440]{1,0:T(8,128)(2,1)S(1)}, bf16[48,1440]{1,0:T(8,128)(2,1)S(1)}, u32[]{:S(2)}, u32[]{:S(2)}) collective-permute-start(bf16[48,1440]{1,0:T(8,128)(2,1)S(1)} %get-tuple-element.536), channel_id=1, source_target_pairs={{0,64},{64,128},{128,192},{192,0},{1,65},{65,129},{129,193},{193,1... | collective-permute-start | bytes 414728 | tf_op jit(solution)/shard_map/while/body/eval_jaxpr/ppermute | solution.py:151
  152.7 6.3 %collective-permute-start = (bf16[48,1440]{1,0:T(8,128)(2,1)S(1)}, bf16[48,1440]{1,0:T(8,128)(2,1)S(1)}, u32[]{:S(2)}, u32[]{:S(2)}) collective-permute-start(bf16[48,1440]{1,0:T(8,128)(2,1)S(1)} %get-tuple-element.536), channel_id=1, source_target_pairs={{0,64},{64,128},{128,192},{192,0},{1,65},{65,129},{129,193},{193,1... | collective-permute-start | bytes 414728 | tf_op jit(solution)/shard_map/while/body/eval_jaxpr/ppermute | solution.py:151
  225.9 6.3 %collective-permute-start = (bf16[48,1440]{1,0:T(8,128)(2,1)S(1)}, bf16[48,1440]{1,0:T(8,128)(2,1)S(1)}, u32[]{:S(2)}, u32[]{:S(2)}) collective-permute-start(bf16[48,1440]{1,0:T(8,128)(2,1)S(1)} %get-tuple-element.536), channel_id=1, source_target_pairs={{0,64},{64,128},{128,192},{192,0},{1,65},{65,129},{129,193},{193,1... | collective-permute-start | bytes 414728 | tf_op jit(solution)/shard_map/while/body/eval_jaxpr/ppermute | solution.py:151
  299.1 6.3 %collective-permute-start = (bf16[48,1440]{1,0:T(8,128)(2,1)S(1)}, bf16[48,1440]{1,0:T(8,128)(2,1)S(1)}, u32[]{:S(2)}, u32[]{:S(2)}) collective-permute-start(bf16[48,1440]{1,0:T(8,128)(2,1)S(1)} %get-tuple-element.536), channel_id=1, source_target_pairs={{0,64},{64,128},{128,192},{192,0},{1,65},{65,129},{129,193},{193,1... | collective-permute-start | bytes 414728 | tf_op jit(solution)/shard_map/while/body/eval_jaxpr/ppermute | solution.py:151
  372.2 6.3 %collective-permute-start = (bf16[48,1440]{1,0:T(8,128)(2,1)S(1)}, bf16[48,1440]{1,0:T(8,128)(2,1)S(1)}, u32[]{:S(2)}, u32[]{:S(2)}) collective-permute-start(bf16[48,1440]{1,0:T(8,128)(2,1)S(1)} %get-tuple-element.536), channel_id=1, source_target_pairs={{0,64},{64,128},{128,192},{192,0},{1,65},{65,129},{129,193},{193,1... | collective-permute-start | bytes 414728 | tf_op jit(solution)/shard_map/while/body/eval_jaxpr/ppermute | solution.py:151
  445.4 0.8 copy-start

commit v4 on v3

--- a/solution.py
+++ b/solution.py
@@ -6,6 +6,7 @@
 from jax.sharding import PartitionSpec as P
 
 CHUNK = 2
+CAP = 2
 ROW_STEP = 32
 COLUMN_BLOCKS = ((0, 1024), (1024, 1920), (1920, 2880))
 
@@ -50,6 +51,60 @@
     down_copy.wait()
     result = jnp.dot(activated[...], down_here[...], preferred_element_type=jnp.float32)
     out_ref[...] = result.reshape(experts_n, per_expert, width).astype(jnp.bfloat16)
+
+
+def place_kernel(section_ref, incoming_ref, fresh_ref, gain_ref, target_ref, out_ref, stream_ref):
+    experts_n, per_expert, width = out_ref.shape
+    slots = experts_n * per_expert
+    rows_n = incoming_ref.shape[0]
+    stream = jnp.where(
+        section_ref[0] == 0, fresh_ref[...].astype(jnp.float32), incoming_ref[...].astype(jnp.float32)
+    )
+    stream_ref[...] = stream.astype(jnp.bfloat16)
+    scale = lax.rsqrt(jnp.mean(stream * stream, axis=-1, keepdims=True) + 1e-05)
+    normed = (stream * scale * gain_ref[...]).astype(jnp.bfloat16)
+    slot_ids = lax.broadcasted_iota(jnp.int32, (slots, rows_n), 0)
+    placing = jnp.zeros((slots, rows_n), jnp.float32)
+    for choice in range(target_ref.shape[0]):
+        placing += jnp.where(slot_ids == target_ref[choice : choice + 1, :], 1.0, 0.0)
+    outgoing = jnp.dot(placing.astype(jnp.bfloat16), normed, preferred_element_type=jnp.float32)
+    out_ref[...] = outgoing.reshape(experts_n, per_expert, width).astype(jnp.bfloat16)
+
+
+def place(section, incoming, fresh, gain, target_columns, experts_n):
+    rows_n, width = incoming.shape
+    per_expert = CHUNK * CAP
+    whole = pl.BlockSpec(memory_space=pltpu.VMEM)
+    return pl.pallas_call(
+        place_kernel,
+        out_shape=(
+            jax.ShapeDtypeStruct((experts_n, per_expert, width), jnp.bfloat16),
+            jax.ShapeDtypeStruct((rows_n, width), jnp.bfloat16),
+        ),
+        in_specs=[pl.BlockSpec(memory_space=pltpu.SMEM)] + [whole] * 4,
+        out_specs=(whole, whole),
+        compiler_params=pltpu.CompilerParams(vmem_limit_bytes=16 << 20),
+    )(section, incoming, fresh, gain, target_columns)
+
+
+def combine_kernel(returned_ref, mixing_ref, stream_ref, out_ref):
+    experts_n, per_expert, width = returned_ref.shape
+    rows_n = stream_ref.shape[0]
+    rows = returned_ref[...].reshape(experts_n * per_expert, width)
+    mixed = jnp.dot(mixing_ref[...], rows, preferred_element_type=jnp.float32)
+    total = mixed[:rows_n] + (mixed[rows_n : 2 * rows_n] + mixed[2 * rows_n :])
+    out_ref[...] = (stream_ref[...].astype(jnp.float32) + total).astype(jnp.bfloat16)
+
+
+def combine(returned, mixing, stream):
+    whole = pl.BlockSpec(memory_space=pltpu.VMEM)
+    return pl.pallas_call(
+        combine_kernel,
+        out_shape=jax.ShapeDtypeStruct(stream.shape, stream.dtype),
+        in_specs=[whole] * 3,
+        out_specs=whole,
+        compiler_params=pltpu.CompilerParams(vmem_limit_bytes=16 << 20),
+    )(returned, mixing, stream)
 
 
 def expert_ffn(arrived, gate_up_w, down_w):
@@ -86,10 +141,8 @@
     section_index = lax.axis_index("section")
     chunk_count = micro_count // CHUNK
     rows_n = CHUNK * token_count
-    cap = max(2, token_count * chosen * 3 // (2 * experts_n))
-    per_expert = CHUNK * cap
-    slots = experts_n * per_expert
-    gain_row = norm_gain[0]
+    per_expert = CHUNK * CAP
+    slots = experts_n * per_expert
     gate_up_w = gate_up[0, 0]
     down_w = down[0, 0]
 
@@ -98,7 +151,7 @@
     same = (pairs[:, :, None] == pairs[:, None, :]) & (order[None, :] < order[:, None])[None]
     rank = jnp.sum(same.astype(jnp.int32), axis=-1)
     block = (jnp.arange(micro_count, dtype=jnp.int32) % CHUNK)[:, None]
-    target = (pairs * per_expert + block * cap + rank).reshape(chunk_count, rows_n, chosen)
+    target = (pairs * per_expert + block * CAP + rank).reshape(chunk_count, rows_n, chosen)
     fixed_point = route_weights[0].astype(jnp.float32)
     shares = fixed_point / jnp.sum(fixed_point, axis=-1, keepdims=True)
     shares = shares.reshape(chunk_count, rows_n, chosen)
@@ -106,57 +159,51 @@
 
     slot_ids = jnp.arange(slots, dtype=jnp.int32)
 
-    def step(tick_number, stream, results, ahead):
+    section_scalar = section_index.reshape(1).astype(jnp.int32)
+
+    def step(tick_number, incoming, fresh_input, results, ahead):
         chunk_here = tick_number - section_index
         clamped = jnp.clip(chunk_here, 0, chunk_count - 1)
         target_rows = lax.dynamic_index_in_dim(target, clamped, 0, keepdims=False)
         share_rows = lax.dynamic_index_in_dim(shares, clamped, 0, keepdims=False)
-        hits = [slot_ids[:, None] == target_rows[None, :, k] for k in range(chosen)]
-        placing = sum(h.astype(jnp.float32) for h in hits).astype(jnp.bfloat16)
         mixing = sum(
             jnp.where(slot_ids[None, :] == target_rows[:, k : k + 1], share_rows[:, k : k + 1], 0.0)
             for k in range(chosen)
         )
         mixing = jnp.concatenate(split_three(mixing), axis=0)
-
-        widened = stream.astype(jnp.float32)
-        scale = lax.rsqrt(jnp.mean(widened * widened, axis=-1, keepdims=True) + 1e-05)
-        normed = (widened * scale * gain_row[None, :]).astype(jnp.bfloat16)
-        outgoing = jnp.dot(placing, normed, preferred_element_type=jnp.float32).astype(jnp.bfloat16)
-        outgoing = outgoing.reshape(experts_n, per_expert, width)
+        outgoing, stream = place(
+            section_scalar, incoming, fresh_input, norm_gain, target_rows.T, experts_n
+        )
         active = jnp.logical_and(chunk_here >= 0, chunk_here < chunk_count)
         kept = lax.dynamic_index_in_dim(results, clamped, 0, keepdims=False)
-        place = clamped.astype(jnp.uint32)
+        place_at = clamped.astype(jnp.uint32)
         if ahead:
-            outgoing, mixing, kept, active, place = lax.optimization_barrier(
-                (outgoing, mixing, kept, active, place)
+            outgoing, mixing, kept, active, place_at = lax.optimization_barrier(
+                (outgoing, mixing, kept, active, place_at)
             )
         arrived = lax.all_to_all(outgoing, "expert", split_axis=0, concat_axis=0, tiled=True)
         computed = expert_ffn(arrived, gate_up_w, down_w)
         returned = lax.all_to_all(computed, "expert", split_axis=0, concat_axis=0, tiled=True)
-        returned_rows = returned.reshape(slots, width)
-        mixed = jnp.dot(mixing, returned_rows, preferred_element_type=jnp.float32)
-        mixed = mixed.reshape(3, rows_n, width)
-        output_rows = (widened + (mixed[0] + (mixed[1] + mixed[2]))).astype(jnp.bfloat16)
-
+        output_rows = combine(returned, mixing, stream)
         results = lax.dynamic_update_slice(
             results,
             jnp.where(active, output_rows, kept)[None],
-            (place, jnp.uint32(0), jnp.uint32(0)),
+            (place_at, jnp.uint32(0), jnp.uint32(0)),
         )
         return output_rows, results
 
     def relayed(tick_number, carried):
         previous, results = carried
-        incoming = lax.ppermute(previous, "section", [(s, (s + 1) % sections) for s in range(sections)])
+        incoming = lax.ppermute(
+            previous, "section", [(s, (s + 1) % sections) for s in range(sections)]
+        )
         fresh_input = lax.dynamic_index_in_dim(
             chunks, jnp.minimum(tick_number, chunk_count - 1), 0, keepdims=False
         )
-        return step(tick_number, jnp.where(section_index == 0, fresh_input, incoming), results, True)
+        return step(tick_number, incoming, fresh_input, results, True)
 
     results = jnp.zeros((chunk_count, rows_n, width), jnp.bfloat16)
-    first_stream = jnp.where(section_index == 0, chunks[0], jnp.zeros_like(chunks[0]))
-    carried = step(0, first_stream, results, False)
+    carried = step(0, jnp.zeros_like(chunks[0]), chunks[0], results, False)
     carried = lax.fori_loop(1, chunk_count + sections - 1, relayed, carried)
     return carried[1].reshape(1, micro_count, token_count, width)
 

time: 447 us -> 440 us (0.984)
  Pallas kernels: 39.6 us -> 45.1 us
  matrix products: 4.49 us -> 0 us
    pallas_call x0 -> x12, Pallas kernels: none -> 5.58 us  [the longest x6 3.83 us: place(): pl.pallas_call(place_kernel, out_shape=(jax.ShapeDtypeStruct((experts_n,...]
    squeeze x5, local copies, waits for them, and re-layouts: 0.1 us -> 4.7 us  [step(): kept = lax.dynamic_index_in_dim(results, clamped, 0, keepdims=False)]
    dot_general x12 -> x0, matrix products: 4.49 us -> none  [the longest x6 2.79 us: step(): jnp.dot(placing, normed, preferred_element_type=jnp.float32)]
  transfers between devices with their start and end apart: 6 -> 6, of which waited for: 6 -> 6; matrix products, arithmetic and copies ran while one was open for 0% -> 1% of each run, Pallas kernels for 0% -> 0%
where the time goes in v4:
time: 440 us; the launch traced here: 439 us
  blocking collectives  329 us (75%)
  waiting for transfers between devices  46.5 us (11%)
  Pallas kernels  45.1 us (10%)
  local copies, waits for them, and re-layouts  8.11 us (2%)
  starting transfers between devices  7.86 us (2%)
    all_to_all x6, blocking collectives, step(): lax.all_to_all(outgoing, 'expert', split_axis=0, concat_axis=0, tiled=True)  184 us
    all_to_all x5, blocking collectives, step(): lax.all_to_all(computed, 'expert', split_axis=0, concat_axis=0, tiled=True)  145 us
    pallas_call x6, Pallas kernels, expert_ffn(): pl.pallas_call(ffn_kernel, out_shape=jax.ShapeDtypeStruct(arrived.shape,...  39.6 us
    ppermute x5, waiting for transfers between devices, relayed(): lax.ppermute(previous, 'section', [(s, (s + 1) % sections) for s in range...  24 us
    all_to_all x1, waiting for transfers between devices, step(): lax.all_to_all(computed, 'expert', split_axis=0, concat_axis=0, tiled=True)  22.5 us
  transfers between devices with their start and end apart: 6, of which 6 were waited for; matrix products, arithmetic and copies ran while one was open for 1% of the time, Pallas kernels for 0%

profile of v4, /device:TPU:1, one launch (start us, length us, event | category | flops | bytes accessed | tf_op | source)
XLA Modules:
  0.0 439.0 jit_solution(7141956276687812765)
XLA Ops:
  3.4 1.2 shard_map.64
  4.6 35.9 %all_to_all.26.x_ref = bf16[64,4,1440]{2,1,0:T(4,128)(2,1)S(1)} all-to-all(bf16[64,4,1440]{2,1,0:T(4,128)(2,1)S(1)} %get-tuple-element.214), channel_id=1, replica_groups=mesh['section'=4,'expert'=64] {'expert'}, dimensions={0} | all-to-all | bytes 1474560 | tf_op jit(solution)/shard_map/all_to_all | solution.py:184
  40.5 7.3 %shard_map.65 = bf16[64,4,1440]{2,1,0:T(4,128)(2,1)} custom-call(bf16[64,4,1440]{2,1,0:T(4,128)(2,1)S(1)} %all_to_all.26.x_ref, bf16[1440,2880]{1,0:T(8,128)(2,1)} %bitcast.84, bf16[1440,1440]{1,0:T(8,128)(2,1)} %bitcast.86), custom_call_target="tpu_custom_call" | custom-call | tf_op jit(solution)/shard_map/pallas_call | solution.py:116
  47.8 6.2 %all-to-all-start.3 = ((bf16[64,4,1440]{2,1,0:T(4,128)(2,1)}), bf16[64,4,1440]{2,1,0:T(4,128)(2,1)S(1)}, u32[]{:S(2)}, u32[]{:S(2)}) async-start(bf16[64,4,1440]{2,1,0:T(4,128)(2,1)} %shard_map.65), calls=%async_computation.3 | async-start | bytes 1572864 | tf_op jit(solution)/shard_map/all_to_all | solution.py:186
  54.5 22.5 %all-to-all-done.3.returned_ref = bf16[64,4,1440]{2,1,0:T(4,128)(2,1)S(1)} async-done(((bf16[64,4,1440]{2,1,0:T(4,128)(2,1)}), bf16[64,4,1440]{2,1,0:T(4,128)(2,1)S(1)}, u32[]{:S(2)}, u32[]{:S(2)}) %all-to-all-start.3) | async-done | bytes 737312 | tf_op jit(solution)/shard_map/all_to_all | solution.py:186
  77.4 360.9 %while.17 = (s32[]{:T(128)}, bf16[48,1440]{1,0:T(8,128)(2,1)S(1)}, bf16[3,48,1440]{2,1,0:T(8,128)(2,1)S(1)}, bf16[3,48,1440]{2,1,0:T(8,128)(2,1)}, s32[]{:T(128)...) while((s32[]{:T(128)}, bf16[48,1440]{1,0:T(8,128)(2,1)S(1)}, ...), condition=%wide.region_3.4_spmd.clone.clone, body=%wide.region_2.3_spmd.clone.clone.sunk | while | flops 511501 | bytes 4726585 | solution.py:207
  77.4 1.3 collective-permute-start
  78.7 0.9 dynamic-slice_bitcast_fusion.3
  79.8 3.9 collective-permute-done.incoming_ref
  84.2 29.6 %all_to_all.27.x_ref = bf16[64,4,1440]{2,1,0:T(4,128)(2,1)S(1)} all-to-all(bf16[64,4,1440]{2,1,0:T(4,128)(2,1)S(1)} %get-tuple-element.454), channel_id=1, replica_groups=mesh['section'=4,'expert'=64] {'expert'}, dimensions={0} | all-to-all | bytes 1474560 | tf_op jit(solution)/shard_map/while/body/eval_jaxpr/all_to_all | solution.py:184
  113.8 6.4 %eval_jaxpr.16 = bf16[64,4,1440]{2,1,0:T(4,128)(2,1)S(1)} custom-call(bf16[64,4,1440]{2,1,0:T(4,128)(2,1)S(1)} %all_to_all.27.x_ref, bf16[1440,2880]{1,0:T(8,128)(2,1)} %get-tuple-element.499.gate_up_ref, bf16[1440,1440]{1,0:T(8,128)(2,1)} %get-tuple-element.500.down_ref), custom_call_target="tpu_custom_call" | custom-call | tf_op jit(solution)/shard_map/while/body/eval_jaxpr/pallas_call | solution.py:116
  120.3 28.9 %all_to_all.28.returned_ref = bf16[64,4,1440]{2,1,0:T(4,128)(2,1)S(1)} all-to-all(bf16[64,4,1440]{2,1,0:T(4,128)(2,1)S(1)} %eval_jaxpr.16), channel_id=1, replica_groups=mesh['section'=4,'expert'=64] {'expert'}, dimensions={0} | all-to-all | bytes 1474560 | tf_op jit(solution)/shard_map/while/body/eval_jaxpr/all_to_all | solution.py:186
  149.7 0.9 dynamic-slice_bitcast_fusion.3
  150.8 5.0 %collective-permute-done.incoming_ref = bf16[48,1440]{1,0:T(8,128)(2,1)S(1)} collective-permute-done((bf16[48,1440]{1,0:T(8,128)(2,1)S(1)}, bf16[48,1440]{1,0:T(8,128)(2,1)S(1)}, u32[]{:S(2)}, u32[]{:S(2)}) %collective-permute-start) | collective-permute-done | bytes 138272 | tf_op jit(solution)/shard_map/while/body/eval_jaxpr/ppermute | solution.py:197
  156.4 29.6 %all_to_all.27.x_ref = bf16[64,4,1440]{2,1,0:T(4,128)(2,1)S(1)} all-to-all(bf16[64,4,1440]{2,1,0:T(4,128)(2,1)S(1)} %get-tuple-element.454), channel_id=1, replica_groups=mesh['section'=4,'expert'=64] {'expert'}, dimensions={0} | all-to-all | bytes 1474560 | tf_op jit(solution)/shard_map/while/body/eval_jaxpr/all_to_all | solution.py:184
  186.0 6.4 %eval_jaxpr.16 = bf16[64,4,1440]{2,1,0:T(4,128)(2,1)S(1)} custom-call(bf16[64,4,1440]{2,1,0:T(4,128)(2,1)S(1)} %all_to_all.27.x_ref, bf16[1440,2880]{1,0:T(8,128)(2,1)} %get-tuple-element.499.gate_up_ref, bf16[1440,1440]{1,0:T(8,128)(2,1)} %get-tuple-element.500.down_ref), custom_call_target="tpu_custom_call" | custom-call | tf_op jit(solution)/shard_map/while/body/eval_jaxpr/pallas_call | solution.py:116
  192.4 28.9 %all_to_all.28.returned_ref = bf16[64,4,1440]{2,1,0:T(4,128)(2,1)S(1)} all-to-all(bf16[64,4,1440]{2,1,0:T(4,128)(2,1)S(1)} %eval_jaxpr.16), channel_id=1, replica_groups=mesh['section'=4,'expert'=64] {'expert'}, dimensions={0} | all-to-all | bytes 1474560 | tf_op jit(solution)/shard_map/while/body/eval_jaxpr/all_to_all | solution.py:186
  221.9 0.9 dynamic-slice_bitcast_fusion.3
  223.0 5.0 %collective-permute-done.incoming_ref = bf16[48,1440]{1,0:T(8,128)(2,1)S(1)} collective-permute-done((bf16[48,1440]{1,0:T(8,128)(2,1)S(1)}, bf16[48,1440]{1,0:T(8,128)(2,1)S(1)}, u32[]{:S(2)}, u32[]{:S(2)}) %collective-permute-start) | collective-permute-done | bytes 138272 | tf_op jit(solution)/shard_map/while/body/eval_jaxpr/ppermute | solution.py:197
  228.6 29.6 %all_to_all.27.x_ref = bf16[64,4,1440]{2,1,0:T(4,128)(2,1)S(1)} all-to-all(bf16[64,4,1440]{2,1,0:T(4,128)(2,1)S(1)} %get-tuple-element.454), channel_id=1, replica_groups=mesh['section'=4,'expert'=64] {'expert'}, dimensions={0} | all-to-all | bytes 1474560 | tf_op jit(solution)/shard_map/while/body/eval_jaxpr/all_to_all | solution.py:184
  258.2 6.4 %eval_jaxpr.16 = bf16[64,4,1440]{2,1,0:T(4,128)(2,1)S(1)} custom-call(bf16[64,4,1440]{2,1,0:T(4,128)(2,1)S(1)} %all_to_all.27.x_ref, bf16[1440,2880]{1,0:T(8,128)(2,1)} %get-tuple-element.499.gate_up_ref, bf16[1440,1440]{1,0:T(8,128)(2,1)} %get-tuple-element.500.down_ref), custom_call_target="tpu_custom_call" | custom-call | tf_op jit(solution)/shard_map/while/body/eval_jaxpr/pallas_call | solution.py:116
  264.6 28.9 %all_to_all.28.returned_ref = bf16[64,4,1440]{2,1,0:T(4,128)(2,1)S(1)} all-to-all(bf16[64,4,1440]{2,1,0:T(4,128)(2,1)S(1)} %eval_jaxpr.16), channel_id=1, replica_groups=mesh['section'=4,'expert'=64] {'expert'}, dimensions={0} | all-to-all | bytes 1474560 | tf_op jit(solution)/shard_map/while/body/eval_jaxpr/all_to_all | solution.py:186
  294.1 0.9 dynamic-slice_bitcast_fusion.3
  295.2 5.0 %collective-permute-done.incoming_ref = bf16[48,1440]{1,0:T(8,128)(2,1)S(1)} collective-permute-done((bf16[48,1440]{1,0:T(8,128)(2,1)S(1)}, bf16[48,1440]{1,0:T(8,128)(2,1)S(1)}, u32[]{:S(2)}, u32[]{:S(2)}) %collective-permute-start) | collective-permute-done | bytes 138272 | tf_op jit(solution)/shard_map/while/body/eval_jaxpr/ppermute | solution.py:197
  300.7 29.6 %all_to_all.27.x_ref = bf16[64,4,1440]{2,1,0:T(4,128)(2,1)S(1)} all-to-all(bf16[64,4,1440]{2,1,0:T(4,128)(2,1)S(1)} %get-tuple-element.454), channel_id=1, replica_groups=mesh['section'=4,'expert'=64] {'expert'}, dimensions={0} | all-to-all | bytes 1474560 | tf_op jit(solution)/shard_map/while/body/eval_jaxpr/all_to_all | solution.py:184
  330.3 6.4 %eval_jaxpr.16 = bf16[64,4,1440]{2,1,0:T(4,128)(2,1)S(1)} custom-call(bf16[64,4,1440]{2,1,0:T(4,128)(2,1)S(1)} %all_to_all.27.x_ref, bf16[1440,2880]{1,0:T(8,128)(2,1)} %get-tuple-element.499.gate_up_ref, bf16[1440,1440]{1,0:T(8,128)(2,1)} %get-tuple-element.500.down_ref), custom_call_target="tpu_custom_call" | custom-call | tf_op jit(solution)/shard_map/while/body/eval_jaxpr/pallas_call | solution.py:116
  336.8 28.9 %all_to_all.28.returned_ref = bf16[64,4,1440]{2,1,0:T(4,128)(2,1)S(1)} all-to-all(bf16[64,4,1440]{2,1,0:T(4,128)(2,1)S(1)} %eval_jaxpr.16), channel_id=1, replica_groups=mesh['section'=4,'expert'=64] {'expert'}, dimensions={0} | all-to-all | bytes 1474560 | tf_op jit(solution)/shard_map/while/body/eval_jaxpr/all_to_all | solution.py:186
  366.3 0.9 dynamic-slice_bitcast_fusion.3
  367.4 5.0 %collective-permute-done.incoming_ref = bf16[48,1440]{1,0:T(8,128)(2,1)S(1)} collective-permute-done((bf16[48,1440]{1,0:T(8,128)(2,1)S(1)}, bf16[48,1440]{1,0:T(8,128)(2,1)S(1)}, u32[]{:S(2)}, u32[]{:S(2)}) %collective-permute-start) | collective-permute-done | bytes 138272 | tf_op jit(solution)/shard_map/while/body/eval_jaxpr/ppermute | solution.py:197
  372.9 29.6 %all_to_all.27.x_ref = bf16[64,4,1440]{2,1,0:T(4,128)(2,1)S(1)} all-to-all(bf16[64,4,1440]{2,1,0:T(4,128)(2,1)S(1)} %get-tuple-element.454), channel_id=1, replica_groups=mesh['section'=4,'expert'=64] {'expert'}, dimensions={0} | all-to-all | bytes 1474560 | tf_op jit(solution)/shard_map/while/body/eval_jaxpr/all_to_all | solution.py:184
  402.5 6.4 %eval_jaxpr.16 = bf16[64,4,1440]{2,1,0:T(4,128)(2,1)S(1)} custom-call(bf16[64,4,1440]{2,1,0:T(4,128)(2,1)S(1)} %all_to_all.27.x_ref, bf16[1440,2880]{1,0:T(8,128)(2,1)} %get-tuple-element.499.gate_up_ref, bf16[1440,1440]{1,0:T(8,128)(2,1)} %get-tuple-element.500.down_ref), custom_call_target="tpu_custom_call" | custom-call | tf_op jit(solution)/shard_map/while/body/eval_jaxpr/pallas_call | solution.py:116
  409.0 28.9 %all_to_all.28.returned_ref = bf16[64,4,1440]{2,1,0:T(4,128)(2,1)S(1)} all-to-all(bf16[64,4,1440]{2,1,0:T(4,128)(2,1)S(1)} %eval_jaxpr.16), channel_id=1, replica_groups=mesh['section'=4,'expert'=64] {'expert'}, dimensions={0} | all-to-all | bytes 1474560 | tf_op jit(solution)/shard_map/while/body/eval_jaxpr/all_to_all | solution.py:186
  (85 shorter events, 10.2 us)
Async XLA Ops:
  4.6 49.5 %copy-start.2 = (s32[1,6,24,4]{2,3,1,0:T(4,128)S(1)}, s32[1,6,24,4]{2,3,1,0:T(4,128)}, u32[]{:S(2)}) copy-start(s32[1,6,24,4]{2,3,1,0:T(4,128)} %param.13) | copy-start | bytes 6916
  40.5 36.9 %copy-start.1 = (f32[1,1440]{1,0:T(1,128)S(1)}, f32[1,1440]{1,0:T(1,128)}, u32[]{:S(2)}) copy-start(f32[1,1440]{1,0:T(1,128)} %gain_ref.1) | copy-start | bytes 17284
  47.8 29.2 %all-to-all-start.3 = ((bf16[64,4,1440]{2,1,0:T(4,128)(2,1)}), bf16[64,4,1440]{2,1,0:T(4,128)(2,1)S(1)}, u32[]{:S(2)}, u32[]{:S(2)}) async-start(bf16[64,4,1440]{2,1,0:T(4,128)(2,1)} %shard_map.65), calls=%async_computation.3 | async-start | bytes 1572864 | tf_op jit(solution)/shard_map/all_to_all | solution.py:186
  77.4 6.3 %collective-permute-start = (bf16[48,1440]{1,0:T(8,128)(2,1)S(1)}, bf16[48,1440]{1,0:T(8,128)(2,1)S(1)}, u32[]{:S(2)}, u32[]{:S(2)}) collective-permute-start(bf16[48,1440]{1,0:T(8,128)(2,1)S(1)} %get-tuple-element.476), channel_id=1, source_target_pairs={{0,64},{64,128},{128,192},{192,0},{1,65},{65,129},{129,193},{193,1... | collective-permute-start | bytes 414728 | tf_op jit(solution)/shard_map/while/body/eval_jaxpr/ppermute | solution.py:197
  149.6 6.3 %collective-permute-start = (bf16[48,1440]{1,0:T(8,128)(2,1)S(1)}, bf16[48,1440]{1,0:T(8,128)(2,1)S(1)}, u32[]{:S(2)}, u32[]{:S(2)}) collective-permute-start(bf16[48,1440]{1,0:T(8,128)(2,1)S(1)} %get-tuple-element.476), channel_id=1, source_target_pairs={{0,64},{64,128},{128,192},{192,0},{1,65},{65,129},{129,193},{193,1... | collective-permute-start | bytes 414728 | tf_op jit(solution)/shard_map/while/body/eval_jaxpr/ppermute | solution.py:197
  221.7 6.3 %collective-permute-start = (bf16[48,1440]{1,0:T(8,128)(2,1)S(1)}, bf16[48,1440]{1,0:T(8,128)(2,1)S(1)}, u32[]{:S(2)}, u32[]{:S(2)}) collective-permute-start(bf16[48,1440]{1,0:T(8,128)(2,1)S(1)} %get-tuple-element.476), channel_id=1, source_target_pairs={{0,64},{64,128},{128,192},{192,0},{1,65},{65,129},{129,193},{193,1... | collective-permute-start | bytes 414728 | tf_op jit(solution)/shard_map/while/body/eval_jaxpr/ppermute | solution.py:197
  293.9 6.3 %collective-permute-start = (bf16[48,1440]{1,0:T(8,128)(2,1)S(1)}, bf16[48,1440]{1,0:T(8,128)(2,1)S(1)}, u32[]{:S(2)}, u32[]{:S(2)}) collective-permute-start(bf16[48,1440]{1,0:T(8,128)(2,1)S(1)} %get-tuple-element.476), channel_id=1, source_target_pairs={{0,64},{64,128},{128,192},{192,0},{1,65},{65,129},{129,193},{193,1... | collective-permute-start | bytes 414728 | tf_op jit(solution)/shard_map/while/body/eval_jaxpr/ppermute | solution.py:197
  366.1 6.3 %collective-permute-start = (bf16[48,1440]{1,0:T(8,128)(2,1)S(1)}, bf16[48,1440]{1,0:T(8,128)(2,1)S(1)}, u32[]{:S(2)}, u32[]{:S(2)}) collective-permute-start(bf16[48,1440]{1,0:T(8,128)(2,1)S(1)} %get-tuple-element.476), channel_id=1, source_target_pairs={{0,64},{64,128},{128,192},{192,0},{1,65},{65,129},{129,193},{193,1... | collective-permute-start | bytes 414728 | tf_op jit(solution)/shard_map/while/body/eval_jaxpr/ppermute | solution.py:197
  438.3 0.8 copy-start

commit v5 on v4

--- a/solution.py
+++ b/solution.py
@@ -146,7 +146,7 @@
     gate_up_w = gate_up[0, 0]
     down_w = down[0, 0]
 
-    pairs = routes[0].reshape(micro_count, token_count * chosen)
+    pairs = lax.optimization_barrier(routes[0].reshape(micro_count, token_count * chosen))
     order = jnp.arange(token_count * chosen, dtype=jnp.int32)
     same = (pairs[:, :, None] == pairs[:, None, :]) & (order[None, :] < order[:, None])[None]
     rank = jnp.sum(same.astype(jnp.int32), axis=-1)

time: 440 us -> 439 us (level)
  no operation moved by 1% of the time
where the time goes in v5:
time: 439 us; the launch traced here: 438 us
  blocking collectives  329 us (75%)
  waiting for transfers between devices  46.4 us (11%)
  Pallas kernels  45.2 us (10%)
  local copies, waits for them, and re-layouts  7.94 us (2%)
  starting transfers between devices  7.86 us (2%)
    all_to_all x6, blocking collectives, step(): lax.all_to_all(outgoing, 'expert', split_axis=0, concat_axis=0, tiled=True)  184 us
    all_to_all x5, blocking collectives, step(): lax.all_to_all(computed, 'expert', split_axis=0, concat_axis=0, tiled=True)  145 us
    pallas_call x6, Pallas kernels, expert_ffn(): pl.pallas_call(ffn_kernel, out_shape=jax.ShapeDtypeStruct(arrived.shape,...  39.6 us
    ppermute x5, waiting for transfers between devices, relayed(): lax.ppermute(previous, 'section', [(s, (s + 1) % sections) for s in range...  24 us
    all_to_all x1, waiting for transfers between devices, step(): lax.all_to_all(computed, 'expert', split_axis=0, concat_axis=0, tiled=True)  22.4 us
  transfers between devices with their start and end apart: 6, of which 6 were waited for; matrix products, arithmetic and copies ran while one was open for 1% of the time, Pallas kernels for 0%

profile of v5, /device:TPU:1, one launch (start us, length us, event | category | flops | bytes accessed | tf_op | source)
XLA Modules:
  0.0 438.1 jit_solution(17516258154061143376)
XLA Ops:
  2.5 1.2 shard_map.64
  3.7 35.9 %all_to_all.26.x_ref = bf16[64,4,1440]{2,1,0:T(4,128)(2,1)S(1)} all-to-all(bf16[64,4,1440]{2,1,0:T(4,128)(2,1)S(1)} %get-tuple-element.214), channel_id=1, replica_groups=mesh['section'=4,'expert'=64] {'expert'}, dimensions={0} | all-to-all | bytes 1474560 | tf_op jit(solution)/shard_map/all_to_all | solution.py:184
  39.6 7.3 %shard_map.65 = bf16[64,4,1440]{2,1,0:T(4,128)(2,1)} custom-call(bf16[64,4,1440]{2,1,0:T(4,128)(2,1)S(1)} %all_to_all.26.x_ref, bf16[1440,2880]{1,0:T(8,128)(2,1)} %bitcast.77, bf16[1440,1440]{1,0:T(8,128)(2,1)} %bitcast.79), custom_call_target="tpu_custom_call" | custom-call | tf_op jit(solution)/shard_map/pallas_call | solution.py:116
  46.9 6.2 %all-to-all-start.3 = ((bf16[64,4,1440]{2,1,0:T(4,128)(2,1)}), bf16[64,4,1440]{2,1,0:T(4,128)(2,1)S(1)}, u32[]{:S(2)}, u32[]{:S(2)}) async-start(bf16[64,4,1440]{2,1,0:T(4,128)(2,1)} %shard_map.65), calls=%async_computation.3 | async-start | bytes 1572864 | tf_op jit(solution)/shard_map/all_to_all | solution.py:186
  53.7 22.4 %all-to-all-done.3.returned_ref = bf16[64,4,1440]{2,1,0:T(4,128)(2,1)S(1)} async-done(((bf16[64,4,1440]{2,1,0:T(4,128)(2,1)}), bf16[64,4,1440]{2,1,0:T(4,128)(2,1)S(1)}, u32[]{:S(2)}, u32[]{:S(2)}) %all-to-all-start.3) | async-done | bytes 737312 | tf_op jit(solution)/shard_map/all_to_all | solution.py:186
  76.5 360.9 %while.17 = (s32[]{:T(128)}, bf16[48,1440]{1,0:T(8,128)(2,1)S(1)}, bf16[3,48,1440]{2,1,0:T(8,128)(2,1)S(1)}, bf16[3,48,1440]{2,1,0:T(8,128)(2,1)}, s32[]{:T(128)...) while((s32[]{:T(128)}, bf16[48,1440]{1,0:T(8,128)(2,1)S(1)}, ...), condition=%wide.region_3.4_spmd.clone.clone, body=%wide.region_2.3_spmd.clone.clone.sunk | while | flops 511501 | bytes 4727353 | solution.py:207
  76.5 1.3 collective-permute-start
  77.8 0.9 dynamic-slice_bitcast_fusion.6
  78.9 3.9 collective-permute-done.incoming_ref
  83.3 29.6 %all_to_all.27.x_ref = bf16[64,4,1440]{2,1,0:T(4,128)(2,1)S(1)} all-to-all(bf16[64,4,1440]{2,1,0:T(4,128)(2,1)S(1)} %get-tuple-element.460), channel_id=1, replica_groups=mesh['section'=4,'expert'=64] {'expert'}, dimensions={0} | all-to-all | bytes 1474560 | tf_op jit(solution)/shard_map/while/body/eval_jaxpr/all_to_all | solution.py:184
  112.9 6.4 %eval_jaxpr.16 = bf16[64,4,1440]{2,1,0:T(4,128)(2,1)S(1)} custom-call(bf16[64,4,1440]{2,1,0:T(4,128)(2,1)S(1)} %all_to_all.27.x_ref, bf16[1440,2880]{1,0:T(8,128)(2,1)} %get-tuple-element.505.gate_up_ref, bf16[1440,1440]{1,0:T(8,128)(2,1)} %get-tuple-element.506.down_ref), custom_call_target="tpu_custom_call" | custom-call | tf_op jit(solution)/shard_map/while/body/eval_jaxpr/pallas_call | solution.py:116
  119.4 28.9 %all_to_all.28.returned_ref = bf16[64,4,1440]{2,1,0:T(4,128)(2,1)S(1)} all-to-all(bf16[64,4,1440]{2,1,0:T(4,128)(2,1)S(1)} %eval_jaxpr.16), channel_id=1, replica_groups=mesh['section'=4,'expert'=64] {'expert'}, dimensions={0} | all-to-all | bytes 1474560 | tf_op jit(solution)/shard_map/while/body/eval_jaxpr/all_to_all | solution.py:186
  148.8 0.9 dynamic-slice_bitcast_fusion.6
  149.9 5.0 %collective-permute-done.incoming_ref = bf16[48,1440]{1,0:T(8,128)(2,1)S(1)} collective-permute-done((bf16[48,1440]{1,0:T(8,128)(2,1)S(1)}, bf16[48,1440]{1,0:T(8,128)(2,1)S(1)}, u32[]{:S(2)}, u32[]{:S(2)}) %collective-permute-start) | collective-permute-done | bytes 138272 | tf_op jit(solution)/shard_map/while/body/eval_jaxpr/ppermute | solution.py:197
  155.5 29.6 %all_to_all.27.x_ref = bf16[64,4,1440]{2,1,0:T(4,128)(2,1)S(1)} all-to-all(bf16[64,4,1440]{2,1,0:T(4,128)(2,1)S(1)} %get-tuple-element.460), channel_id=1, replica_groups=mesh['section'=4,'expert'=64] {'expert'}, dimensions={0} | all-to-all | bytes 1474560 | tf_op jit(solution)/shard_map/while/body/eval_jaxpr/all_to_all | solution.py:184
  185.1 6.4 %eval_jaxpr.16 = bf16[64,4,1440]{2,1,0:T(4,128)(2,1)S(1)} custom-call(bf16[64,4,1440]{2,1,0:T(4,128)(2,1)S(1)} %all_to_all.27.x_ref, bf16[1440,2880]{1,0:T(8,128)(2,1)} %get-tuple-element.505.gate_up_ref, bf16[1440,1440]{1,0:T(8,128)(2,1)} %get-tuple-element.506.down_ref), custom_call_target="tpu_custom_call" | custom-call | tf_op jit(solution)/shard_map/while/body/eval_jaxpr/pallas_call | solution.py:116
  191.5 28.9 %all_to_all.28.returned_ref = bf16[64,4,1440]{2,1,0:T(4,128)(2,1)S(1)} all-to-all(bf16[64,4,1440]{2,1,0:T(4,128)(2,1)S(1)} %eval_jaxpr.16), channel_id=1, replica_groups=mesh['section'=4,'expert'=64] {'expert'}, dimensions={0} | all-to-all | bytes 1474560 | tf_op jit(solution)/shard_map/while/body/eval_jaxpr/all_to_all | solution.py:186
  221.0 0.9 dynamic-slice_bitcast_fusion.6
  222.1 5.0 %collective-permute-done.incoming_ref = bf16[48,1440]{1,0:T(8,128)(2,1)S(1)} collective-permute-done((bf16[48,1440]{1,0:T(8,128)(2,1)S(1)}, bf16[48,1440]{1,0:T(8,128)(2,1)S(1)}, u32[]{:S(2)}, u32[]{:S(2)}) %collective-permute-start) | collective-permute-done | bytes 138272 | tf_op jit(solution)/shard_map/while/body/eval_jaxpr/ppermute | solution.py:197
  227.7 29.6 %all_to_all.27.x_ref = bf16[64,4,1440]{2,1,0:T(4,128)(2,1)S(1)} all-to-all(bf16[64,4,1440]{2,1,0:T(4,128)(2,1)S(1)} %get-tuple-element.460), channel_id=1, replica_groups=mesh['section'=4,'expert'=64] {'expert'}, dimensions={0} | all-to-all | bytes 1474560 | tf_op jit(solution)/shard_map/while/body/eval_jaxpr/all_to_all | solution.py:184
  257.3 6.4 %eval_jaxpr.16 = bf16[64,4,1440]{2,1,0:T(4,128)(2,1)S(1)} custom-call(bf16[64,4,1440]{2,1,0:T(4,128)(2,1)S(1)} %all_to_all.27.x_ref, bf16[1440,2880]{1,0:T(8,128)(2,1)} %get-tuple-element.505.gate_up_ref, bf16[1440,1440]{1,0:T(8,128)(2,1)} %get-tuple-element.506.down_ref), custom_call_target="tpu_custom_call" | custom-call | tf_op jit(solution)/shard_map/while/body/eval_jaxpr/pallas_call | solution.py:116
  263.7 28.9 %all_to_all.28.returned_ref = bf16[64,4,1440]{2,1,0:T(4,128)(2,1)S(1)} all-to-all(bf16[64,4,1440]{2,1,0:T(4,128)(2,1)S(1)} %eval_jaxpr.16), channel_id=1, replica_groups=mesh['section'=4,'expert'=64] {'expert'}, dimensions={0} | all-to-all | bytes 1474560 | tf_op jit(solution)/shard_map/while/body/eval_jaxpr/all_to_all | solution.py:186
  293.2 0.9 dynamic-slice_bitcast_fusion.6
  294.3 5.0 %collective-permute-done.incoming_ref = bf16[48,1440]{1,0:T(8,128)(2,1)S(1)} collective-permute-done((bf16[48,1440]{1,0:T(8,128)(2,1)S(1)}, bf16[48,1440]{1,0:T(8,128)(2,1)S(1)}, u32[]{:S(2)}, u32[]{:S(2)}) %collective-permute-start) | collective-permute-done | bytes 138272 | tf_op jit(solution)/shard_map/while/body/eval_jaxpr/ppermute | solution.py:197
  299.8 29.6 %all_to_all.27.x_ref = bf16[64,4,1440]{2,1,0:T(4,128)(2,1)S(1)} all-to-all(bf16[64,4,1440]{2,1,0:T(4,128)(2,1)S(1)} %get-tuple-element.460), channel_id=1, replica_groups=mesh['section'=4,'expert'=64] {'expert'}, dimensions={0} | all-to-all | bytes 1474560 | tf_op jit(solution)/shard_map/while/body/eval_jaxpr/all_to_all | solution.py:184
  329.4 6.4 %eval_jaxpr.16 = bf16[64,4,1440]{2,1,0:T(4,128)(2,1)S(1)} custom-call(bf16[64,4,1440]{2,1,0:T(4,128)(2,1)S(1)} %all_to_all.27.x_ref, bf16[1440,2880]{1,0:T(8,128)(2,1)} %get-tuple-element.505.gate_up_ref, bf16[1440,1440]{1,0:T(8,128)(2,1)} %get-tuple-element.506.down_ref), custom_call_target="tpu_custom_call" | custom-call | tf_op jit(solution)/shard_map/while/body/eval_jaxpr/pallas_call | solution.py:116
  335.9 28.9 %all_to_all.28.returned_ref = bf16[64,4,1440]{2,1,0:T(4,128)(2,1)S(1)} all-to-all(bf16[64,4,1440]{2,1,0:T(4,128)(2,1)S(1)} %eval_jaxpr.16), channel_id=1, replica_groups=mesh['section'=4,'expert'=64] {'expert'}, dimensions={0} | all-to-all | bytes 1474560 | tf_op jit(solution)/shard_map/while/body/eval_jaxpr/all_to_all | solution.py:186
  365.4 0.9 dynamic-slice_bitcast_fusion.6
  366.5 5.0 %collective-permute-done.incoming_ref = bf16[48,1440]{1,0:T(8,128)(2,1)S(1)} collective-permute-done((bf16[48,1440]{1,0:T(8,128)(2,1)S(1)}, bf16[48,1440]{1,0:T(8,128)(2,1)S(1)}, u32[]{:S(2)}, u32[]{:S(2)}) %collective-permute-start) | collective-permute-done | bytes 138272 | tf_op jit(solution)/shard_map/while/body/eval_jaxpr/ppermute | solution.py:197
  372.0 29.6 %all_to_all.27.x_ref = bf16[64,4,1440]{2,1,0:T(4,128)(2,1)S(1)} all-to-all(bf16[64,4,1440]{2,1,0:T(4,128)(2,1)S(1)} %get-tuple-element.460), channel_id=1, replica_groups=mesh['section'=4,'expert'=64] {'expert'}, dimensions={0} | all-to-all | bytes 1474560 | tf_op jit(solution)/shard_map/while/body/eval_jaxpr/all_to_all | solution.py:184
  401.6 6.4 %eval_jaxpr.16 = bf16[64,4,1440]{2,1,0:T(4,128)(2,1)S(1)} custom-call(bf16[64,4,1440]{2,1,0:T(4,128)(2,1)S(1)} %all_to_all.27.x_ref, bf16[1440,2880]{1,0:T(8,128)(2,1)} %get-tuple-element.505.gate_up_ref, bf16[1440,1440]{1,0:T(8,128)(2,1)} %get-tuple-element.506.down_ref), custom_call_target="tpu_custom_call" | custom-call | tf_op jit(solution)/shard_map/while/body/eval_jaxpr/pallas_call | solution.py:116
  408.1 28.9 %all_to_all.28.returned_ref = bf16[64,4,1440]{2,1,0:T(4,128)(2,1)S(1)} all-to-all(bf16[64,4,1440]{2,1,0:T(4,128)(2,1)S(1)} %eval_jaxpr.16), channel_id=1, replica_groups=mesh['section'=4,'expert'=64] {'expert'}, dimensions={0} | all-to-all | bytes 1474560 | tf_op jit(solution)/shard_map/while/body/eval_jaxpr/all_to_all | solution.py:186
  (81 shorter events, 9.4 us)
Async XLA Ops:
  3.7 49.6 %copy-start.2 = (s32[1,6,24,4]{2,3,1,0:T(4,128)S(1)}, s32[1,6,24,4]{2,3,1,0:T(4,128)}, u32[]{:S(2)}) copy-start(s32[1,6,24,4]{2,3,1,0:T(4,128)} %param.13) | copy-start | bytes 6916
  39.6 36.9 %copy-start.1 = (f32[1,1440]{1,0:T(1,128)S(1)}, f32[1,1440]{1,0:T(1,128)}, u32[]{:S(2)}) copy-start(f32[1,1440]{1,0:T(1,128)} %gain_ref.1) | copy-start | bytes 17284
  46.9 29.2 %all-to-all-start.3 = ((bf16[64,4,1440]{2,1,0:T(4,128)(2,1)}), bf16[64,4,1440]{2,1,0:T(4,128)(2,1)S(1)}, u32[]{:S(2)}, u32[]{:S(2)}) async-start(bf16[64,4,1440]{2,1,0:T(4,128)(2,1)} %shard_map.65), calls=%async_computation.3 | async-start | bytes 1572864 | tf_op jit(solution)/shard_map/all_to_all | solution.py:186
  76.5 6.3 %collective-permute-start = (bf16[48,1440]{1,0:T(8,128)(2,1)S(1)}, bf16[48,1440]{1,0:T(8,128)(2,1)S(1)}, u32[]{:S(2)}, u32[]{:S(2)}) collective-permute-start(bf16[48,1440]{1,0:T(8,128)(2,1)S(1)} %get-tuple-element.482), channel_id=1, source_target_pairs={{0,64},{64,128},{128,192},{192,0},{1,65},{65,129},{129,193},{193,1... | collective-permute-start | bytes 414728 | tf_op jit(solution)/shard_map/while/body/eval_jaxpr/ppermute | solution.py:197
  148.7 6.3 %collective-permute-start = (bf16[48,1440]{1,0:T(8,128)(2,1)S(1)}, bf16[48,1440]{1,0:T(8,128)(2,1)S(1)}, u32[]{:S(2)}, u32[]{:S(2)}) collective-permute-start(bf16[48,1440]{1,0:T(8,128)(2,1)S(1)} %get-tuple-element.482), channel_id=1, source_target_pairs={{0,64},{64,128},{128,192},{192,0},{1,65},{65,129},{129,193},{193,1... | collective-permute-start | bytes 414728 | tf_op jit(solution)/shard_map/while/body/eval_jaxpr/ppermute | solution.py:197
  220.8 6.3 %collective-permute-start = (bf16[48,1440]{1,0:T(8,128)(2,1)S(1)}, bf16[48,1440]{1,0:T(8,128)(2,1)S(1)}, u32[]{:S(2)}, u32[]{:S(2)}) collective-permute-start(bf16[48,1440]{1,0:T(8,128)(2,1)S(1)} %get-tuple-element.482), channel_id=1, source_target_pairs={{0,64},{64,128},{128,192},{192,0},{1,65},{65,129},{129,193},{193,1... | collective-permute-start | bytes 414728 | tf_op jit(solution)/shard_map/while/body/eval_jaxpr/ppermute | solution.py:197
  293.0 6.3 %collective-permute-start = (bf16[48,1440]{1,0:T(8,128)(2,1)S(1)}, bf16[48,1440]{1,0:T(8,128)(2,1)S(1)}, u32[]{:S(2)}, u32[]{:S(2)}) collective-permute-start(bf16[48,1440]{1,0:T(8,128)(2,1)S(1)} %get-tuple-element.482), channel_id=1, source_target_pairs={{0,64},{64,128},{128,192},{192,0},{1,65},{65,129},{129,193},{193,1... | collective-permute-start | bytes 414728 | tf_op jit(solution)/shard_map/while/body/eval_jaxpr/ppermute | solution.py:197
  365.2 6.3 %collective-permute-start = (bf16[48,1440]{1,0:T(8,128)(2,1)S(1)}, bf16[48,1440]{1,0:T(8,128)(2,1)S(1)}, u32[]{:S(2)}, u32[]{:S(2)}) collective-permute-start(bf16[48,1440]{1,0:T(8,128)(2,1)S(1)} %get-tuple-element.482), channel_id=1, source_target_pairs={{0,64},{64,128},{128,192},{192,0},{1,65},{65,129},{129,193},{193,1... | collective-permute-start | bytes 414728 | tf_op jit(solution)/shard_map/while/body/eval_jaxpr/ppermute | solution.py:197
  437.4 0.8 copy-start
